TPU v7x, 128 devices: a whole 4x4x4 slice. The times are simulated.
128 devices in a mesh: gx: 8 (over x_hi, z), gy: 16 (over x_lo, y, core).
Axes of the slice: x: 4 (x_hi: 2, x_lo: 2; x = x_hi * 2 + x_lo), y: 4, z: 4, core: 2. Of those that a mesh axis runs over, the one named last changes fastest.
Arguments:
- positions: bfloat16 [64, 128, 3, 128], P('gx', 'gy'), may hold values from 0 to 1
- features: bfloat16 [64, 128, 256, 128], P('gx', 'gy'), may hold values from -6 to 6
- lever: float32 [64, 128, 3, 128], P('gx', 'gy'), may hold values from -4 to 4
- partner: int32 [64, 128, 6], P('gx', 'gy'), may hold values from 0 to 8, as said below
- body_slot: int32 [64, 128, 128], P('gx', 'gy'), may hold values from 0 to 127
- owner_dir: int32 [64, 128, 128], P('gx', 'gy'), may hold values from 0 to 8, as said below
- body_pose: float32 [8, 16, 7, 128], P('gx', 'gy'), as said below
- body_motion: float32 [8, 16, 6, 128], P('gx', 'gy'), may hold values from -5 to 5
- body_inverse: float32 [8, 16, 4, 128], P('gx', 'gy'), may hold values from 0.1 to 1
- weight_u: bfloat16 [512, 256], replicated, may hold values from -0.375 to 0.375
- weight_v: bfloat16 [128, 256], replicated, may hold values from -0.375 to 0.375
- radial_rate: float32 [4], replicated, may hold values from 0.5 to 4
Outputs:
- moved: float32 [64, 128, 3, 128], P('gx', 'gy')
- body_next: float32 [8, 16, 13, 128], P('gx', 'gy')
Inputs may be any that keep to these rules, and one draw needn't show every extreme that they name: `partner`: each tile's 6 codes are distinct; code 3 (a + 1) + (b + 1) names the tile a tiles along the first and b along the second dimension, a, b in -1, 0, 1. `owner_dir`: code 3 (a + 1) + (b + 1) names the domain a, b domains away; a is -1 only in a domain's first row of 8 tiles and 1 only in its last, b likewise for its 8 columns. `body_pose`: rows 3 to 6 are unit quaternions with a positive first entry.
All inputs are finite; a program needn't handle non-finite values.
Results may differ from a plain program's by a relative error of at most 0.0023.
Values may be sent and summed in bfloat16 or wider, within the bound.
A program may use at most 128 MiB of HBM per device.

v0:
```python
import jax
import jax.numpy as jnp
from jax import lax
from jax.sharding import PartitionSpec as P

STEP_DT = 0.25
CUT_SQUARE = 4.0


def from_behind(block, axis, distance):
    devices = range(lax.axis_size(axis))
    route = [((i - distance) % len(devices), i) for i in devices]
    return lax.ppermute(block, axis, route)


def padded_2(value, sides, width):
    for axis, dim in sides:
        devices, length = (lax.axis_size(axis), value.shape[dim])
        up = [(i, (i + 1) % devices) for i in range(devices)]
        down = [(j, i) for i, j in up]
        last = lax.slice_in_dim(value, length - width, length, axis=dim)
        leading = lax.slice_in_dim(value, 0, width, axis=dim)
        before = lax.ppermute(last, axis, up)
        after = lax.ppermute(leading, axis, down)
        value = jnp.concatenate([before, value, after], axis=dim)
    return value


def rotation(quat):
    qw, qa, qb, qc = (quat[0], quat[1], quat[2], quat[3])
    first = jnp.stack(
        [1 - 2 * (qb * qb + qc * qc), 2 * (qa * qb - qw * qc), 2 * (qa * qc + qw * qb)]
    )
    second = jnp.stack(
        [2 * (qa * qb + qw * qc), 1 - 2 * (qa * qa + qc * qc), 2 * (qb * qc - qw * qa)]
    )
    third = jnp.stack(
        [2 * (qa * qc - qw * qb), 2 * (qb * qc + qw * qa), 1 - 2 * (qa * qa + qb * qb)]
    )
    return jnp.stack([first, second, third])


def integrate(pose, motion, inverse, totals):
    centre = pose[0:3]
    quat = pose[3:7]
    new_vel = motion[0:3] + STEP_DT * inverse[0] * totals[0:3]
    new_centre = centre + STEP_DT * new_vel
    new_ang = motion[3:6] + STEP_DT * totals[3:6]
    rot_old = rotation(quat)
    body_frame = jnp.sum(rot_old * new_ang[:, None], axis=0) * inverse[1:4]
    omega = jnp.sum(rot_old * body_frame[None, :], axis=1)
    scalar = -jnp.sum(omega * quat[1:4], axis=0)
    vector = quat[0] * omega + jnp.cross(omega, quat[1:4], axis=0)
    stepped = quat + 0.5 * STEP_DT * jnp.concatenate([scalar[None], vector], axis=0)
    new_quat = stepped / jnp.sqrt(jnp.sum(stepped * stepped, axis=0))
    rot_new = rotation(new_quat)
    relative = jnp.sum(rot_new[:, None, :] * rot_old[None, :, :], axis=2)
    next_state = jnp.concatenate([new_centre, new_quat, new_vel, new_ang], axis=0)
    packed = jnp.concatenate(
        [STEP_DT * new_vel, relative.reshape((9,) + relative.shape[2:])], axis=0
    )
    return (next_state, packed)


def tile_forces(u_row, p_row, v_part, p_part, offset, radial_rate):
    differ = p_row[:, :, :, None] - p_part[:, :, None, :] - offset[:, :, None, None]
    radius_sq = jnp.sum(differ * differ, axis=1)
    envelope = jnp.square(jnp.maximum(1.0 - radius_sq / CUT_SQUARE, 0.0))
    scores = jnp.einsum("mkha,mhb->mkab", u_row, v_part, preferred_element_type=jnp.float32)
    radial = jnp.exp(-radial_rate[None, :, None, None] * radius_sq[:, None])
    couple = envelope * jnp.sum(radial * scores, axis=1) / v_part.shape[1]
    weight_sum = jnp.sum(couple, axis=2)
    pulled = jnp.einsum("mab,mcb->mca", couple, p_part, precision=lax.Precision.HIGHEST)
    return (p_row - offset[:, :, None]) * weight_sum[:, None, :] - pulled


def pick_partner(three_rows, off_x, off_y, tiles_y):
    shape_mask = (-1,) + (1,) * (three_rows.ndim - 2)
    sel_left = (off_y == -1).reshape(shape_mask)
    sel_mid = (off_y == 0).reshape(shape_mask)
    per_row = []
    for row in range(3):
        left = three_rows[row, 0:tiles_y]
        middle = three_rows[row, 1 : tiles_y + 1]
        right = three_rows[row, 2 : tiles_y + 2]
        per_row.append(jnp.where(sel_left, left, jnp.where(sel_mid, middle, right)))
    sel_up = (off_x == -1).reshape(shape_mask)
    sel_same = (off_x == 0).reshape(shape_mask)
    return jnp.where(sel_up, per_row[0], jnp.where(sel_same, per_row[1], per_row[2]))


def along_gy(partial_sums, offset_by):
    return from_behind(partial_sums, "gy", offset_by)


def along_gx(partial_sums, offset_by):
    return from_behind(partial_sums, "gx", offset_by)


def local(
    positions,
    features,
    lever,
    partner,
    body_slot,
    owner_dir,
    body_pose,
    body_motion,
    body_inverse,
    weight_u,
    weight_v,
    radial_rate,
):
    tiles_x, tiles_y = (positions.shape[0], positions.shape[1])
    tile_len = positions.shape[3]
    width_h = weight_v.shape[0]
    channels = weight_u.shape[0] // width_h
    slots = body_pose.shape[3]
    u_all = jnp.einsum(
        "gf,xyfb->xygb", weight_u, features, preferred_element_type=jnp.float32
    ).astype(jnp.bfloat16)
    state = jnp.concatenate([positions, features], axis=2)
    padded = padded_2(state, (("gx", 0), ("gy", 1)), 1)
    pad_v = jnp.einsum(
        "hf,xyfb->xyhb", weight_v, padded[:, :, 3:], preferred_element_type=jnp.float32
    ).astype(jnp.bfloat16)
    pad_pos = padded[:, :, 0:3].astype(jnp.float32)

    def row_forces(inputs):
        row_index, u_row, p_row, codes = inputs
        rows_v = lax.dynamic_slice_in_dim(pad_v, row_index, 3, 0)
        rows_p = lax.dynamic_slice_in_dim(pad_pos, row_index, 3, 0)
        total = jnp.zeros((tiles_y, 3, tile_len), jnp.float32)
        for which in range(codes.shape[1]):
            code = codes[:, which]
            off_x = code // 3 - 1
            off_y = code % 3 - 1
            v_part = pick_partner(rows_v, off_x, off_y, tiles_y)
            p_part = pick_partner(rows_p, off_x, off_y, tiles_y)
            offset = jnp.stack([off_x, off_y, jnp.zeros_like(off_x)], axis=1).astype(jnp.float32)
            total = total + tile_forces(u_row, p_row, v_part, p_part, offset, radial_rate)
        return total

    forces = lax.map(
        row_forces,
        (
            jnp.arange(tiles_x, dtype=jnp.int32),
            u_all.reshape(tiles_x, tiles_y, channels, width_h, tile_len),
            positions.astype(jnp.float32),
            partner,
        ),
    )
    torque = jnp.cross(lever, forces, axis=2)
    terms = jnp.concatenate([forces, torque], axis=2)
    body_key = (owner_dir * slots + body_slot).reshape(tiles_x, tiles_y * tile_len)
    term_rows = jnp.moveaxis(terms, 2, 1).reshape(tiles_x, 6, tiles_y * tile_len)
    segment_ids = jnp.arange(9 * slots, dtype=jnp.int32)

    def row_sums(inputs):
        keys, term_row = inputs
        onehot = (keys[:, None] == segment_ids[None, :]).astype(jnp.float32)
        return jnp.dot(term_row, onehot, precision=lax.Precision.HIGHEST)

    sums = jnp.sum(lax.map(row_sums, (body_key, term_rows)), axis=0)
    parts = jnp.transpose(sums.reshape(6, 3, 3, slots), (1, 2, 0, 3))
    section_one = parts[:, 1] + along_gy(parts[:, 2], 1) + along_gy(parts[:, 0], -1)
    totals = section_one[1] + along_gx(section_one[2], 1) + along_gx(section_one[0], -1)
    next_state, packed = integrate(body_pose[0, 0], body_motion[0, 0], body_inverse[0, 0], totals)
    beside_all = padded_2(packed[None, None], (("gx", 0), ("gy", 1)), 1)
    table = jnp.transpose(beside_all, (2, 0, 1, 3)).reshape(12, 9 * slots)

    def row_lookup(keys):
        onehot = (keys[:, None] == segment_ids[None, :]).astype(jnp.float32)
        picked = jnp.einsum("gs,bs->gb", table, onehot, precision=lax.Precision.HIGHEST)
        return jnp.moveaxis(picked.reshape(12, tiles_y, tile_len), 0, 1)

    looked = lax.map(row_lookup, body_key)
    rotated = jnp.stack(
        [jnp.sum(looked[:, :, 3 + 3 * row : 6 + 3 * row] * lever, axis=2) for row in range(3)],
        axis=2,
    )
    moved = positions.astype(jnp.float32) + looked[:, :, 0:3] + rotated - lever
    return (moved, next_state[None, None])


def solution(mesh):
    placed = (
        P("gx", "gy", None, None),
        P("gx", "gy", None, None),
        P("gx", "gy", None, None),
        P("gx", "gy", None),
        P("gx", "gy", None),
        P("gx", "gy", None),
        P("gx", "gy", None, None),
        P("gx", "gy", None, None),
        P("gx", "gy", None, None),
        P(),
        P(),
        P(),
    )
    return jax.shard_map(
        local,
        mesh=mesh,
        in_specs=placed,
        out_specs=(P("gx", "gy", None, None), P("gx", "gy", None, None)),
        check_vma=False,
    )
```

profile of v0, /device:TPU:1, one launch (start us, length us, event | category | flops | bytes accessed | tf_op | source)
XLA Modules:
  0.0 671.4 jit_solution(6010888353285829033)
XLA Ops:
  2.5 7.1 %copy.82 = bf16[8,8,256,128]{2,3,1,0:T(8,128)(2,1)} copy(bf16[8,8,256,128]{3,2,1,0:T(8,128)(2,1)} %param.19) | data formatting | bytes 8388608 | tf_op args[1]
  14.7 7.0 %collective-permute-start.1 = (bf16[1,8,259,128]{3,1,2,0:T(8,128)(2,1)}, bf16[1,8,259,128]{3,1,2,0:T(8,128)(2,1)}, u32[]{:S(2)}, u32[]{:S(2)}) collective-permute-start(bf16[1,8,259,128]{3,1,2,0:T(8,128)(2,1)} %copy.84), channel_id=1, source_target_pairs={{16,0},{32,16},{48,32},{64,48},{80,64},{96,80},{112,96},{0,112},{1... | collective-permute-start | bytes 1591304 | tf_op jit(solution)/shard_map/ppermute | solution.py:24
  22.9 7.8 %convert_bitcast_fusion = bf16[8,8,512,128]{2,3,1,0:T(8,128)(2,1)} fusion(bf16[8,8,256,128]{3,2,1,0:T(8,128)(2,1)} %param.19, bf16[512,256]{1,0:T(8,128)(2,1)S(1)} %copy-done), kind=kOutput, calls=%fused_computation.335 | convolution fusion | flops 2151677952 | bytes 12845056 | tf_op jit(solution)/shard_map/gf,xyfb->xygb/dot_general | solution.py:119
  32.0 12.6 %reshape.1800 = bf16[8,8,4,128,128]{3,2,4,1,0:T(4,128)(2,1)} reshape(bf16[8,8,512,128]{2,3,1,0:T(8,128)(2,1)} %convert_bitcast_fusion) | data formatting | bytes 16777216 | tf_op jit(solution)/shard_map/reshape | solution.py:148
  49.8 3.4 pad_maximum_fusion.16
  62.1 6.7 %collective-permute-done.3 = bf16[10,1,259,128]{3,2,1,0:T(8,128)(2,1)} collective-permute-done((bf16[10,1,259,128]{3,2,1,0:T(8,128)(2,1)}, bf16[10,1,259,128]{3,2,1,0:T(8,128)(2,1)}, u32[]{:S(2)}, u32[]{:S(2)}) %collective-permute-start.3) | collective-permute-done | bytes 663072 | tf_op jit(solution)/shard_map/ppermute | solution.py:24
  73.3 3.6 pad_maximum_fusion.10
  77.8 6.0 convert_bitcast_fusion.1
  83.9 4.0 copy.91
  90.0 498.8 %while.35 = (s32[]{:T(128)}, f32[8,8,3,128]{3,2,1,0:T(4,128)}, f32[8,8,3,128]{3,1,2,0:T(8,128)}, s32[8,8,6]{1,0,2:T(8,128)}, s32[8]{0:T(128)}, /*index=5*/f32[10...) while((s32[]{:T(128)}, f32[8,8,3,128]{3,2,1,0:T(4,128)}, ...), condition=%wide.region_19.20_spmd, body=%wide.region_0.19_spmd.sunk | while | flops 867648384 | bytes 68705072 | solution.py:144
  131.1 3.2 multiply_reduce_fusion.26
  193.5 3.2 multiply_reduce_fusion.26
  255.8 3.2 multiply_reduce_fusion.26
  318.2 3.2 multiply_reduce_fusion.26
  380.5 3.2 multiply_reduce_fusion.26
  442.9 3.2 multiply_reduce_fusion.26
  505.2 3.2 multiply_reduce_fusion.26
  567.6 3.2 multiply_reduce_fusion.26
  591.0 23.9 %while.36 = (s32[]{:T(128)}, f32[8,6,1152]{2,1,0:T(8,128)}, f32[8,6,1024]{2,1,0:T(8,128)S(1)}, s32[8,1024]{1,0:T(8,128)}, s32[]{:T(128)}) while((s32[]{:T(128)}, f32[8,6,1152]{2,1,0:T(8,128)}, f32[8,6,1024]{2,1,0:T(8,128)S(1)}, s32[8,1024]{1,0:T(8,128)}, s32[]{:T(128)}) %tuple.235), condition=%wide.region_21.22_spmd.clone, body=%wide.region_20.21_spmd.clone.sunk | while | flops 86114304 | bytes 83017 | solution.py:164
  619.3 5.7 collective-permute-start.7
  626.3 5.2 collective-permute-start.9
  632.3 5.3 collective-permute-done.8
  637.6 7.0 %collective-permute-start.11 = (f32[3,1,12,128]{3,2,1,0:T(8,128)S(1)}, f32[3,1,12,128]{3,2,1,0:T(8,128)S(1)}, u32[]{:S(2)}, u32[]{:S(2)}) collective-permute-start(f32[3,1,12,128]{3,2,1,0:T(8,128)S(1)} %pad_maximum_fusion.19), channel_id=1, source_target_pairs={{1,0},{2,1},{3,2},{4,3},{5,4},{6,5},{7,6},{8,7},{9,8},{10,9},{11,1... | collective-permute-start | bytes 55304 | tf_op jit(solution)/shard_map/ppermute | solution.py:24
  646.0 24.6 %while.37 = (s32[]{:T(128)}, f32[8,8,12,128]{3,1,2,0:T(8,128)S(1)}, s32[8,1024]{1,0:T(8,128)}, f32[12,1152]{1,0:T(8,128)S(1)}, s32[]{:T(128)}) while((s32[]{:T(128)}, f32[8,8,12,128]{3,1,2,0:T(8,128)S(1)}, s32[8,1024]{1,0:T(8,128)}, f32[12,1152]{1,0:T(8,128)S(1)}, s32[]{:T(128)}) %tuple.236), condition=%wide.region_29.30_spmd.clone, body=%wide.region_28.29_spmd.clone.sunk | while | flops 171048960 | bytes 346189 | solution.py:177
  (1508 shorter events, 539.9 us)
Async XLA Ops:
  2.5 70.8 %copy-start.2 = (bf16[8,8,3,128]{2,3,1,0:T(8,128)(2,1)}, bf16[8,8,3,128]{2,3,1,0:T(8,128)(2,1)S(1)}, u32[]{:S(2)}) copy-start(bf16[8,8,3,128]{2,3,1,0:T(8,128)(2,1)S(1)} %copy.81) | copy-start | bytes 147460
  14.7 31.1 %collective-permute-start.1 = (bf16[1,8,259,128]{3,1,2,0:T(8,128)(2,1)}, bf16[1,8,259,128]{3,1,2,0:T(8,128)(2,1)}, u32[]{:S(2)}, u32[]{:S(2)}) collective-permute-start(bf16[1,8,259,128]{3,1,2,0:T(8,128)(2,1)} %copy.84), channel_id=1, source_target_pairs={{16,0},{32,16},{48,32},{64,48},{80,64},{96,80},{112,96},{0,112},{1... | collective-permute-start | bytes 1591304 | tf_op jit(solution)/shard_map/ppermute | solution.py:24
  22.9 24.3 %collective-permute-start = (bf16[1,8,259,128]{3,1,2,0:T(8,128)(2,1)}, bf16[1,8,259,128]{3,1,2,0:T(8,128)(2,1)}, u32[]{:S(2)}, u32[]{:S(2)}) collective-permute-start(bf16[1,8,259,128]{3,1,2,0:T(8,128)(2,1)} %copy.83), channel_id=1, source_target_pairs={{0,16},{16,32},{32,48},{48,64},{64,80},{80,96},{96,112},{112,0},{1... | collective-permute-start | bytes 1591304 | tf_op jit(solution)/shard_map/ppermute | solution.py:23
  57.6 11.2 %collective-permute-start.3 = (bf16[10,1,259,128]{3,2,1,0:T(8,128)(2,1)}, bf16[10,1,259,128]{3,2,1,0:T(8,128)(2,1)}, u32[]{:S(2)}, u32[]{:S(2)}) collective-permute-start(bf16[10,1,259,128]{3,2,1,0:T(8,128)(2,1)} %copy.88), channel_id=1, source_target_pairs={{1,0},{2,1},{3,2},{4,3},{5,4},{6,5},{7,6},{8,7},{9,8},{10,9},{11,1... | collective-permute-start | bytes 1989128 | tf_op jit(solution)/shard_map/ppermute | solution.py:24
  58.6 12.5 %collective-permute-start.2 = (bf16[10,1,259,128]{3,2,1,0:T(8,128)(2,1)}, bf16[10,1,259,128]{3,2,1,0:T(8,128)(2,1)}, u32[]{:S(2)}, u32[]{:S(2)}) collective-permute-start(bf16[10,1,259,128]{3,2,1,0:T(8,128)(2,1)} %copy.87), channel_id=1, source_target_pairs={{0,1},{1,2},{2,3},{3,4},{4,5},{5,6},{6,7},{7,8},{8,9},{9,10},{10,1... | collective-permute-start | bytes 1989128 | tf_op jit(solution)/shard_map/ppermute | solution.py:23
  590.9 34.1 %copy-start.77 = (f32[1,128]{1,0:T(1,128)S(1)}, f32[1,128]{1,0:T(1,128)}, u32[]{:S(2)}) copy-start(f32[1,128]{1,0:T(1,128)} %get-tuple-element.470) | copy-start | bytes 1540
  590.9 34.1 %copy-start.78 = (f32[1,128]{1,0:T(1,128)S(1)}, f32[1,128]{1,0:T(1,128)}, u32[]{:S(2)}) copy-start(f32[1,128]{1,0:T(1,128)} %get-tuple-element.471) | copy-start | bytes 1540
  590.9 34.1 %copy-start.82 = (f32[1,128]{1,0:T(1,128)S(1)}, f32[1,128]{1,0:T(1,128)}, u32[]{:S(2)}) copy-start(f32[1,128]{1,0:T(1,128)} %get-tuple-element.475) | copy-start | bytes 1540
  590.9 34.1 %copy-start.50 = (f32[1,1,7,128]{3,1,2,0:T(1,128)S(1)}, f32[1,1,7,128]{3,1,2,0:T(1,128)}, u32[]{:S(2)}) copy-start(f32[1,1,7,128]{3,1,2,0:T(1,128)} %param.24) | copy-start | bytes 10756
  590.9 34.1 %copy-start.51 = (f32[1,1,3,128]{3,1,2,0:T(1,128)S(1)}, f32[1,1,3,128]{3,1,2,0:T(1,128)}, u32[]{:S(2)}) copy-start(f32[1,1,3,128]{3,1,2,0:T(1,128)} %get-tuple-element.466) | copy-start | bytes 4612
  590.9 35.0 %copy-start.68 = (f32[1,1,3,128]{3,1,2,0:T(1,128)S(1)}, f32[1,1,3,128]{3,1,2,0:T(1,128)}, u32[]{:S(2)}) copy-start(f32[1,1,3,128]{3,1,2,0:T(1,128)} %get-tuple-element.465) | copy-start | bytes 4612
  590.9 35.0 %copy-start.69 = (f32[1,1,3,128]{3,1,2,0:T(1,128)S(1)}, f32[1,1,3,128]{3,1,2,0:T(1,128)}, u32[]{:S(2)}) copy-start(f32[1,1,3,128]{3,1,2,0:T(1,128)} %get-tuple-element.492) | copy-start | bytes 4612
  590.9 35.0 %copy-start.70 = (f32[1,1,3,128]{3,1,2,0:T(1,128)S(1)}, f32[1,1,3,128]{3,1,2,0:T(1,128)}, u32[]{:S(2)}) copy-start(f32[1,1,3,128]{3,1,2,0:T(1,128)} %get-tuple-element.493) | copy-start | bytes 4612
  591.0 35.0 %copy-start.83 = (f32[128]{0:T(128)S(1)}, f32[128]{0:T(128)}, u32[]{:S(2)}) copy-start(f32[128]{0:T(128)} %multiply_bitcast_fusion.6) | copy-start | bytes 1540
  591.0 35.0 %copy-start.75 = (f32[1,1,4,128]{3,2,1,0:T(4,128)S(1)}, f32[1,1,4,128]{3,2,1,0:T(4,128)}, u32[]{:S(2)}) copy-start(f32[1,1,4,128]{3,2,1,0:T(4,128)} %param.26) | copy-start | bytes 6148
  591.0 35.0 %copy-start.76 = (f32[128]{0:T(128)S(1)}, f32[128]{0:T(128)}, u32[]{:S(2)}) copy-start(f32[128]{0:T(128)} %get-tuple-element.467) | copy-start | bytes 1540
  615.8 3.1 collective-permute-start.4
  615.9 3.3 collective-permute-start.5
  619.2 6.6 collective-permute-start.6
  619.3 6.6 collective-permute-start.7
  626.3 6.0 collective-permute-start.9
  631.5 6.1 collective-permute-start.8
  637.6 7.8 %collective-permute-start.11 = (f32[3,1,12,128]{3,2,1,0:T(8,128)S(1)}, f32[3,1,12,128]{3,2,1,0:T(8,128)S(1)}, u32[]{:S(2)}, u32[]{:S(2)}) collective-permute-start(f32[3,1,12,128]{3,2,1,0:T(8,128)S(1)} %pad_maximum_fusion.19), channel_id=1, source_target_pairs={{1,0},{2,1},{3,2},{4,3},{5,4},{6,5},{7,6},{8,7},{9,8},{10,9},{11,1... | collective-permute-start | bytes 55304 | tf_op jit(solution)/shard_map/ppermute | solution.py:24
  644.6 1.3 collective-permute-start.10
  (445 other events, 1392.8 us)
where the time goes:
time: 684 us; the launch traced here: 671 us
  local copies, waits for them, and re-layouts  251 us (37%)
  other arithmetic  177 us (26%)
  matrix products  174 us (25%)
  starting transfers between devices  29.6 us (4%)
  loops' own time  22.9 us (3%)
  waiting for transfers between devices  15.2 us (2%)
    while x928, local copies, waits for them, and re-layouts  133 us
    dot_general x48, matrix products, tile_forces(): jnp.einsum('mkha,mhb->mkab', u_row, v_part, preferred_element_type=jnp.fl...  74.7 us
    dot_general x48, matrix products, tile_forces(): jnp.einsum('mab,mcb->mca', couple, p_part, precision=lax.Precision.HIGHEST)  49.9 us
    dynamic_slice x48, local copies, waits for them, and re-layouts, local(): lax.map(row_forces, (jnp.arange(tiles_x, dtype=jnp.int32), u_all.reshape(...  48.1 us
    select_n x16, other arithmetic, pick_partner(): jnp.where(sel_up, per_row[0], jnp.where(sel_same, per_row[1], per_row[2]))  26.9 us
    reduce_sum x8, other arithmetic, tile_forces(): radius_sq = jnp.sum(differ * differ, axis=1)  25.8 us
    another operation x1, loops' own time, local(): lax.map(row_forces, (jnp.arange(tiles_x, dtype=jnp.int32), u_all.reshape(...  22.7 us
    convert_element_type x16, other arithmetic, row_forces(): jnp.stack([off_x, off_y, jnp.zeros_like(off_x)], axis=1).astype(jnp.float32)  22.5 us
  transfers between devices with their start and end apart: 12, of which 8 were waited for; matrix products, arithmetic and copies ran while one was open for 5% of the time, Pallas kernels for 0%

commit v1 on v0

v1 whole, which is shorter than its diff:
```python
import jax
import jax.numpy as jnp
from jax import lax
from jax.experimental import pallas as pl
from jax.experimental.pallas import tpu as pltpu
from jax.sharding import PartitionSpec as P

STEP_DT = 0.25
LOG2E = 1.4426950408889634
MESH = pl.DeviceIdType.MESH
F32 = jnp.float32
BF16 = jnp.bfloat16
INNER_FIRST = 14
CODES = [c for c in range(9) if c != 4]
MIX = "DUUDUUDUUDUUDUU"


def mm(a, b):
    return jnp.dot(a, b, preferred_element_type=F32)


def mm_nt(a, b):
    return lax.dot_general(a, b, (((1,), (1,)), ((), ())), preferred_element_type=F32)


def split3(value):
    high = value.astype(BF16).astype(F32)
    rest = value - high
    mid = rest.astype(BF16).astype(F32)
    return high, mid, rest - mid


def inner_pair(q):
    i = 1 + q // 3
    j = 1 + 2 * (q % 3)
    return i, j, i, j + 1


def rim_pair(q):
    in_rows = q < 8
    c = q - 8
    i = jnp.where(in_rows, 7 * (q // 4), 1 + 2 * (c % 3))
    j = jnp.where(in_rows, 2 * (q % 4), 7 * (c // 3))
    return i, j, jnp.where(in_rows, i, i + 1), jnp.where(in_rows, j + 1, j)


def row_pair(q):
    i = 7 * (q // 4)
    j = 2 * (q % 4)
    return i, j, i, j + 1


def col_pair(q):
    i = 1 + 2 * (q % 3)
    j = 7 * (q // 3)
    return i, j, i + 1, j


def any_pair(p):
    rim = rim_pair(jnp.clip(p - INNER_FIRST, 0, 13))
    inner = inner_pair(jnp.clip(jnp.where(p < INNER_FIRST, p, p - 14), 0, 17))
    is_rim = (p >= INNER_FIRST) & (p < INNER_FIRST + 14)
    return tuple(jnp.where(is_rim, r, n) for r, n in zip(rim, inner))


def rotation_rows(qw, qa, qb, qc):
    return [
        [1 - 2 * (qb * qb + qc * qc), 2 * (qa * qb - qw * qc), 2 * (qa * qc + qw * qb)],
        [2 * (qa * qb + qw * qc), 1 - 2 * (qa * qa + qc * qc), 2 * (qb * qc - qw * qa)],
        [2 * (qa * qc - qw * qb), 2 * (qb * qc + qw * qa), 1 - 2 * (qa * qa + qb * qb)],
    ]


def kernel(
    codes,
    rates,
    positions,
    features,
    lever_in,
    slot_in,
    owner_in,
    pose_in,
    motion_in,
    inverse_in,
    wu_in,
    wv_in,
    moved,
    body_next,
    pos,
    feat,
    lever,
    slot,
    owner,
    pose,
    motion,
    inverse,
    wu,
    wv,
    vt,
    qf,
    qm,
    rp,
    u,
    oh,
    raw,
    terms,
    acc,
    part_out,
    part_in,
    table,
    table_f32,
    pos_row,
    pos_col,
    pos_corner,
    v_row,
    v_col,
    v_corner,
    s_even,
    s_odd,
    in_sem,
    pos_send,
    pos_recv,
    v_send,
    v_recv,
    part_send,
    part_recv,
    table_send,
    table_recv,
):
    gx, gy = lax.axis_index("gx"), lax.axis_index("gy")
    nx, ny = lax.axis_size("gx"), lax.axis_size("gy")

    def neighbour(code):
        a, b = code // 3 - 1, code % 3 - 1
        return (lax.rem(gx + a + nx, nx), lax.rem(gy + b + ny, ny))

    loads = []

    def load(src, dst):
        copy = pltpu.make_async_copy(src, dst, in_sem.at[len(loads)])
        copy.start()
        loads.append(copy)
        return copy

    got_pos = load(positions, pos)
    got_wv = load(wv_in, wv)
    rim_loads = [
        load(features.at[0], feat.at[0]),
        load(features.at[7], feat.at[7]),
        load(features.at[1:7, 0], feat.at[1:7, 0]),
        load(features.at[1:7, 7], feat.at[1:7, 7]),
    ]
    small_loads = [
        load(slot_in, slot),
        load(owner_in, owner),
        load(lever_in, lever),
        load(pose_in, pose),
        load(motion_in, motion),
        load(inverse_in, inverse),
        load(wu_in, wu),
    ]
    inner_loads = [load(features.at[i, 1:7], feat.at[i, 1:7]) for i in range(1, 7)]

    barrier = pltpu.get_barrier_semaphore()
    for code in CODES:
        pl.semaphore_signal(barrier, inc=1, device_id=neighbour(code), device_id_type=MESH)

    rate_scale = [rates[k] * (-LOG2E) for k in range(4)]
    lead = rate_scale[0]
    ratio = [None] + [rate_scale[k] / lead for k in range(1, 4)]
    four_lead = -4.0 * lead
    final_scale = 1.0 / (2048.0 * lead * lead)
    row8 = lax.broadcasted_iota(jnp.int32, (8, 128), 0)
    zero8 = jnp.zeros((8, 128), F32)

    raw[...] = jnp.zeros_like(raw)
    acc[...] = jnp.zeros_like(acc)
    table_f32[...] = jnp.zeros_like(table_f32)

    def clear(t, carry):
        qf[t] = jnp.zeros((128, 128), BF16)
        return carry

    lax.fori_loop(0, 100, clear, 0)

    got_pos.wait()
    pl.semaphore_wait(barrier, 8)

    def pos_src(a, b):
        if b == 0:
            return pos.at[0 if a < 0 else 7]
        if a == 0:
            return pos.at[:, 0 if b < 0 else 7]
        return pos.at[0 if a < 0 else 7, 0 if b < 0 else 7]

    def v_src(a, b):
        if b == 0:
            return vt.at[pl.ds(11 if a < 0 else 81, 8)]
        if a == 0:
            return None
        return vt.at[(10 if a < 0 else 80) + (1 if b < 0 else 8)]

    def landing(a, b, row_ref, col_ref, corner_ref):
        if b == 0:
            return row_ref.at[1 if a < 0 else 0]
        if a == 0:
            return col_ref.at[1 if b < 0 else 0]
        return corner_ref.at[(2 if a < 0 else 0) + (1 if b < 0 else 0)]

    pos_copies, v_copies = [], []
    for n, code in enumerate(CODES):
        a, b = code // 3 - 1, code % 3 - 1
        pos_copies.append(
            pltpu.make_async_remote_copy(
                src_ref=pos_src(a, b),
                dst_ref=landing(a, b, pos_row, pos_col, pos_corner),
                send_sem=pos_send.at[n],
                recv_sem=pos_recv.at[n],
                device_id=neighbour(code),
                device_id_type=MESH,
            )
        )
    for copy in pos_copies:
        copy.start()

    def pair_features(pair):
        ia, ja, ib, jb = pair
        return jnp.concatenate([feat[ia, ja], feat[ib, jb]], axis=1)

    def project_v(pair):
        ia, ja, ib, jb = pair
        v = mm(wv[...], pair_features(pair)).astype(BF16)
        vt[(ia + 1) * 10 + ja + 1] = v[:, 0:128].T
        vt[(ib + 1) * 10 + jb + 1] = v[:, 128:256].T

    def project_u(pair):
        ia, ja, ib, jb = pair
        both = mm(wu[...], pair_features(pair)).astype(BF16)
        u[ia * 8 + ja] = both[:, 0:128]
        u[ib * 8 + jb] = both[:, 128:256]

    got_wv.wait()
    for copy in rim_loads:
        copy.wait()

    def rim_rows_v(q, carry):
        project_v(row_pair(2 * q))
        project_v(row_pair(2 * q + 1))
        return carry

    def rim_cols_v(q, carry):
        for extra in range(3):
            pair = col_pair(3 * q + extra)
            ia, ja, ib, jb = pair
            project_v(pair)
        return carry

    lax.fori_loop(0, 4, rim_rows_v, 0)
    lax.fori_loop(0, 2, rim_cols_v, 0)

    vt4 = vt.reshape(10, 10, 128, 128)
    for n, code in enumerate(CODES):
        a, b = code // 3 - 1, code % 3 - 1
        src = vt4.at[1:9, 1 if b < 0 else 8] if a == 0 else v_src(a, b)
        v_copies.append(
            pltpu.make_async_remote_copy(
                src_ref=src,
                dst_ref=landing(a, b, v_row, v_col, v_corner),
                send_sem=v_send.at[n],
                recv_sem=v_recv.at[n],
                device_id=neighbour(code),
                device_id_type=MESH,
            )
        )
    for n in sorted(range(8), key=lambda n: (CODES[n] // 3 == 1, CODES[n])):
        v_copies[n].start()

    def partner_tables(index, x3, gi, gj):
        qx, qy, qz = x3[0:1], x3[1:2], x3[2:3]
        ax, ay = qx + gi, qy + gj
        b_high, b_mid, b_low = split3(lead * (ax * ax + ay * ay + qz * qz))
        g0 = jnp.where(row8 < 3, qx, jnp.where(row8 < 6, qy, qz))
        g1 = jnp.where(row8 == 0, qz, jnp.where(row8 < 4, gi, jnp.where(row8 < 7, gj, 0.0)))
        g2 = jnp.where(
            row8 == 0,
            b_high,
            jnp.where(
                row8 == 1,
                b_mid,
                jnp.where(row8 == 2, b_low, jnp.where(row8 < 6, 1.0, 0.0)),
            ),
        )
        stack = jnp.concatenate([g0, g1, g2, zero8], axis=0)
        qf[index, :, 0:32] = stack.T.astype(BF16)
        m0 = jnp.where(
            row8 == 0,
            qx,
            jnp.where(
                row8 == 1,
                qy,
                jnp.where(
                    row8 == 2,
                    qz,
                    jnp.where(
                        row8 == 3,
                        1.0,
                        jnp.where(row8 == 4, gi, jnp.where(row8 == 5, gj, 0.0)),
                    ),
                ),
            ),
        )
        qm[index] = jnp.concatenate([m0, zero8], axis=0).astype(BF16)

    def place(i):
        return i.astype(F32) - 3.5 if not isinstance(i, int) else float(i) - 3.5

    def pick3(first, parts):
        return jnp.where(row8 == first, parts[0], jnp.where(row8 == first + 1, parts[1], parts[2]))

    def own_tables(i, j):
        x3 = pos[i, j].astype(F32)
        gi, gj = place(i), place(j)
        partner_tables((i + 1) * 10 + j + 1, x3, gi, gj)
        ax, ay, az = x3[0:1] + gi, x3[1:2] + gj, x3[2:3]
        xs = split3(-2.0 * lead * ax)
        ys = split3(-2.0 * lead * ay)
        zs = split3(-2.0 * lead * az)
        sq = split3(lead * (ax * ax + ay * ay + az * az))
        g0 = jnp.where(
            row8 < 3,
            pick3(0, xs),
            jnp.where(row8 < 6, pick3(3, ys), jnp.where(row8 == 6, zs[0], zs[1])),
        )
        g1 = jnp.where(
            row8 == 0,
            zs[2],
            jnp.where(row8 < 4, pick3(1, xs), jnp.where(row8 < 7, pick3(4, ys), 0.0)),
        )
        g2 = jnp.where(row8 < 3, 1.0, jnp.where(row8 < 6, pick3(3, sq), 0.0))
        rp[i * 8 + j] = jnp.concatenate([g0, g1, g2, zero8], axis=0).astype(BF16)

    slots = lax.broadcasted_iota(jnp.int32, (128, 128), 0)

    def onehot(i, j):
        here = slot[i, pl.ds(j, 1), :]
        oh[i * 8 + j] = jnp.where(slots == here, 1.0, 0.0).astype(BF16)

    for copy in small_loads:
        copy.wait()

    def prepare(q, carry):
        i = q // 2
        for step in range(4):
            j = 4 * (q % 2) + step
            own_tables(i, j)
            onehot(i, j)
        return carry

    lax.fori_loop(0, 16, prepare, 0)
    for copy in inner_loads:
        copy.wait()

    def inner_v(q, carry):
        project_v(inner_pair(2 * q))
        project_v(inner_pair(2 * q + 1))
        return carry

    lax.fori_loop(0, 9, inner_v, 0)

    def all_u(q, carry):
        for step in range(2):
            p = 2 * q + step
            i, j = p // 4, 2 * (p % 4)
            project_u((i, j, i, j + 1))
        return carry

    lax.fori_loop(0, 16, all_u, 0)

    def partners(i, j):
        found = []
        for n in range(6):
            c = codes[i, j, n]
            found.append(i * 10 + j + c + 7 * ((c * 11) >> 5))
        return found

    zeros96 = jnp.zeros((96, 128), BF16)
    zeros128 = jnp.zeros((128, 128), BF16)

    def scores(p, s):
        ia, ja, ib, jb = any_pair(p)
        pa, pb = partners(ia, ja), partners(ib, jb)
        for x, (t, found) in enumerate(((ia * 8 + ja, pa), (ib * 8 + jb, pb))):
            rows = jnp.concatenate([vt[n] for n in found], axis=0)
            for half in range(2):
                first = u[t, 256 * half : 256 * half + 128, :]
                second = u[t, 256 * half + 128 : 256 * half + 256, :]
                s[2 * x + half] = mm(rows, jnp.concatenate([first, second], axis=1))
                yield
        rows = jnp.concatenate(
            [jnp.concatenate([qf[n], qf[m]], axis=1) for n, m in zip(pa, pb)], axis=0
        )
        right = jnp.concatenate(
            [
                jnp.concatenate([rp[ia * 8 + ja], zeros96, zeros128], axis=0),
                jnp.concatenate([zeros128, rp[ib * 8 + jb], zeros96], axis=0),
            ],
            axis=1,
        )
        s[4] = mm(rows, right)
        yield

    def couples(p, s):
        ia, ja, ib, jb = any_pair(p)
        pa, pb = partners(ia, ja), partners(ib, jb)
        for x, (t, found) in enumerate(((ia * 8 + ja, pa), (ib * 8 + jb, pb))):
            total = None
            for two in range(3):
                couple = []
                for n in (2 * two, 2 * two + 1):
                    rows = slice(n * 128, (n + 1) * 128)
                    t0 = s[4, rows, x * 128 : (x + 1) * 128]
                    mixed = None
                    for k in range(4):
                        score = s[2 * x + k // 2, rows, (k % 2) * 128 : (k % 2 + 1) * 128]
                        term = jnp.exp2(t0 if k == 0 else t0 * ratio[k]) * score
                        mixed = term if mixed is None else mixed + term
                    inside = jnp.maximum(t0 + four_lead, 0.0)
                    couple.append((mixed * (inside * inside)).astype(BF16))
                    yield
                left = jnp.concatenate([qm[found[2 * two]], qm[found[2 * two + 1]]], axis=1)
                got = mm(left, jnp.concatenate(couple, axis=0))
                total = got if total is None else total + got
            raw[pl.ds(pl.multiple_of(t * 8, 8), 8), :] = total[0:8]

    def run(steps):
        for _ in steps:
            pass

    def mixed_run(first, second):
        for which in MIX:
            next(first if which == "D" else second)
        run(first)
        run(second)

    def finish_halo():
        for copy in pos_copies:
            copy.wait_recv()
        for copy in v_copies:
            copy.wait_recv()

        def rows(q, carry):
            side, j = q // 8, q % 8
            index = 90 * side + j + 1
            vt[index] = v_row[side, j]
            partner_tables(index, pos_row[side, j].astype(F32), 9 * side.astype(F32) - 4.5, place(j))
            return carry

        def cols(q, carry):
            side, i = q // 8, q % 8
            index = (i + 1) * 10 + 9 * side
            vt[index] = v_col[side, i]
            partner_tables(index, pos_col[side, i].astype(F32), place(i), 9 * side.astype(F32) - 4.5)
            return carry

        def corners(q, carry):
            si, sj = q // 2, q % 2
            index = 90 * si + 9 * sj
            vt[index] = v_corner[q]
            partner_tables(
                index,
                pos_corner[q].astype(F32),
                9 * si.astype(F32) - 4.5,
                9 * sj.astype(F32) - 4.5,
            )
            return carry

        lax.fori_loop(0, 16, rows, 0)
        lax.fori_loop(0, 16, cols, 0)
        lax.fori_loop(0, 4, corners, 0)

    def force_terms():
        def row(i, carry):
            def strided(c):
                return raw[pl.ds(64 * i + c, 8, stride=8), :]

            weight = strided(3)
            ground = lax.broadcasted_iota(jnp.int32, (8, 128), 0).astype(F32) - 3.5
            px = pos[i, :, 0, :].astype(F32) + place(i)
            py = pos[i, :, 1, :].astype(F32) + ground
            pz = pos[i, :, 2, :].astype(F32)
            lx, ly, lz = lever[i, :, 0, :], lever[i, :, 1, :], lever[i, :, 2, :]
            fx = (px * weight - (strided(0) + strided(4))) * final_scale
            fy = (py * weight - (strided(1) + strided(5))) * final_scale
            fz = (pz * weight - strided(2)) * final_scale
            rows = [fx, fy, fz, ly * fz - lz * fy, lz * fx - lx * fz, lx * fy - ly * fx]
            for c, value in enumerate(rows + [jnp.zeros_like(fx)] * 2):
                terms[pl.ds(64 * i + c, 8, stride=8), :] = value
            return carry

        lax.fori_loop(0, 8, row, 0)

    def two_parts(t):
        value = terms[pl.ds(pl.multiple_of(t * 8, 8), 8), :]
        high = value.astype(BF16).astype(F32)
        return jnp.concatenate([high, value - high], axis=0)

    def pair_onehot(ta, tb):
        return jnp.concatenate([oh[ta], oh[tb]], axis=1)

    def masked_sums(pair, start, count):
        ia, ja, ib, jb = pair
        ta, tb = ia * 8 + ja, ib * 8 + jb
        value = jnp.concatenate([two_parts(ta), two_parts(tb)], axis=1)
        whose = jnp.concatenate([owner[ia, pl.ds(ja, 1), :], owner[ib, pl.ds(jb, 1), :]], axis=1)
        left = [jnp.where(whose == start + c, value, 0.0).astype(BF16) for c in range(count)]
        got = mm_nt(jnp.concatenate(left, axis=0), pair_onehot(ta, tb))
        where = pl.ds(pl.multiple_of(start * 16, 16), count * 16)
        acc[where, :] = acc[where, :] + got

    part_copies = []
    for n, code in enumerate(CODES):
        part_copies.append(
            pltpu.make_async_remote_copy(
                src_ref=part_out.at[code],
                dst_ref=part_in.at[code],
                send_sem=part_send.at[n],
                recv_sem=part_recv.at[n],
                device_id=neighbour(code),
                device_id_type=MESH,
            )
        )

    def send_parts():
        force_terms()

        def rows(q, carry):
            masked_sums(row_pair(q), 3 * (q // 4), 6)
            return carry

        def cols(q, carry):
            masked_sums(col_pair(q), 3 + q // 3, 2)
            return carry

        lax.fori_loop(0, 8, rows, 0)
        lax.fori_loop(0, 6, cols, 0)
        for code in CODES:
            part_out[code] = acc[16 * code : 16 * code + 8, :] + acc[16 * code + 8 : 16 * code + 16, :]
        for copy in part_copies:
            copy.start()

    run(scores(0, s_even))

    def two_pairs(q, carry):
        pl.when(q == INNER_FIRST // 2 - 1)(finish_halo)
        pl.when(q == INNER_FIRST // 2 + 7)(send_parts)
        mixed_run(scores(2 * q + 1, s_odd), couples(2 * q, s_even))
        mixed_run(scores(2 * q + 2, s_even), couples(2 * q + 1, s_odd))
        return carry

    lax.fori_loop(0, 15, two_pairs, 0)
    mixed_run(scores(31, s_odd), couples(30, s_even))
    run(couples(31, s_odd))

    force_terms()

    def inner_sums(q, total):
        for step in range(2):
            ia, ja, ib, jb = inner_pair(2 * q + step)
            ta, tb = ia * 8 + ja, ib * 8 + jb
            value = jnp.concatenate([two_parts(ta), two_parts(tb)], axis=1).astype(BF16)
            total = total + mm_nt(value, pair_onehot(ta, tb))
        return total

    own = lax.fori_loop(0, 9, inner_sums, acc[64:80, :])
    total = own[0:8] + own[8:16]
    for copy in part_copies:
        copy.wait_recv()
    for code in CODES:
        total = total + part_in[code]

    state = pose[0, 0]
    moving = motion[0, 0]
    inv = inverse[0, 0]
    centre = [state[c : c + 1] for c in range(3)]
    quat = [state[c : c + 1] for c in range(3, 7)]
    vel = [moving[c : c + 1] + STEP_DT * inv[0:1] * total[c : c + 1] for c in range(3)]
    ang = [moving[c : c + 1] + STEP_DT * total[c : c + 1] for c in range(3, 6)]
    shift = [STEP_DT * v for v in vel]
    rot = rotation_rows(*quat)
    frame = [
        (rot[0][c] * ang[0] + rot[1][c] * ang[1] + rot[2][c] * ang[2]) * inv[c + 1 : c + 2]
        for c in range(3)
    ]
    omega = [rot[r][0] * frame[0] + rot[r][1] * frame[1] + rot[r][2] * frame[2] for r in range(3)]
    qw, qv = quat[0], quat[1:4]
    change = [
        -(omega[0] * qv[0] + omega[1] * qv[1] + omega[2] * qv[2]),
        qw * omega[0] + (omega[1] * qv[2] - omega[2] * qv[1]),
        qw * omega[1] + (omega[2] * qv[0] - omega[0] * qv[2]),
        qw * omega[2] + (omega[0] * qv[1] - omega[1] * qv[0]),
    ]
    stepped = [q + 0.5 * STEP_DT * d for q, d in zip(quat, change)]
    norm = jnp.sqrt(sum(s * s for s in stepped[1:]) + stepped[0] * stepped[0])
    turned = [s / norm for s in stepped]
    rot_new = rotation_rows(*turned)
    for c in range(3):
        table_f32[c : c + 1, :] = shift[c]
        for r in range(3):
            entry = sum(rot_new[r][k] * rot[c][k] for k in range(3))
            table_f32[8 * (c + 1) + r : 8 * (c + 1) + r + 1, :] = entry
    whole = table_f32[...]
    high = whole.astype(BF16)
    table[256:288, :] = high
    table[288:320, :] = (whole - high.astype(F32)).astype(BF16)
    table_copies = []
    for n, code in enumerate(CODES):
        table_copies.append(
            pltpu.make_async_remote_copy(
                src_ref=table.at[pl.ds(256, 64)],
                dst_ref=table.at[pl.ds((8 - code) * 64, 64)],
                send_sem=table_send.at[n],
                recv_sem=table_recv.at[n],
                device_id=neighbour(code),
                device_id_type=MESH,
            )
        )
    for copy in table_copies:
        copy.start()
    next_rows = [c + s for c, s in zip(centre, shift)] + turned + vel + ang
    for c, value in enumerate(next_rows):
        body_next[0, 0, c : c + 1, :] = value

    def put(i, j, picked):
        x3 = pos[i, j].astype(F32)
        l3 = lever[i, j]
        moved[i, j] = (
            x3
            + picked[0:3]
            + picked[8:11] * l3[0:1]
            + picked[16:19] * l3[1:2]
            + picked[24:27] * l3[2:3]
            - l3
        )

    def move_pair(pair, start, count):
        ia, ja, ib, jb = pair
        ta, tb = ia * 8 + ja, ib * 8 + jb
        if count == 1:
            rows = table[256:320, :]
        else:
            rows = table[pl.ds(pl.multiple_of(start * 64, 64), count * 64), :]
        got = mm(rows, pair_onehot(ta, tb))
        whose = None
        if count > 1:
            whose = jnp.concatenate([owner[ia, pl.ds(ja, 1), :], owner[ib, pl.ds(jb, 1), :]], axis=1)
        picked = None
        for c in range(count):
            one = got[64 * c : 64 * c + 32] + got[64 * c + 32 : 64 * c + 64]
            picked = one if picked is None else jnp.where(whose == start + c, one, picked)
        put(ia, ja, picked[:, 0:128])
        put(ib, jb, picked[:, 128:256])

    def move_inner(q, carry):
        move_pair(inner_pair(2 * q), 4, 1)
        move_pair(inner_pair(2 * q + 1), 4, 1)
        return carry

    lax.fori_loop(0, 9, move_inner, 0)
    for copy in table_copies:
        copy.wait_recv()

    def move_rows(q, carry):
        move_pair(row_pair(q), 3 * (q // 4), 6)
        return carry

    def move_cols(q, carry):
        move_pair(col_pair(2 * q), 3 + (2 * q) // 3, 2)
        move_pair(col_pair(2 * q + 1), 3 + (2 * q + 1) // 3, 2)
        return carry

    lax.fori_loop(0, 8, move_rows, 0)
    lax.fori_loop(0, 3, move_cols, 0)
    for copy in pos_copies + v_copies + part_copies + table_copies:
        copy.wait_send()


def local(
    positions,
    features,
    lever,
    partner,
    body_slot,
    owner_dir,
    body_pose,
    body_motion,
    body_inverse,
    weight_u,
    weight_v,
    radial_rate,
):
    hbm = pl.BlockSpec(memory_space=pl.ANY)
    smem = pl.BlockSpec(memory_space=pltpu.SMEM)
    vmem = pl.BlockSpec(memory_space=pltpu.VMEM)
    dma = pltpu.SemaphoreType.DMA
    like = lambda x: pltpu.VMEM(x.shape, x.dtype)
    return pl.pallas_call(
        kernel,
        out_shape=(
            jax.ShapeDtypeStruct((8, 8, 3, 128), F32),
            jax.ShapeDtypeStruct((1, 1, 13, 128), F32),
        ),
        in_specs=[smem, smem] + [hbm] * 10,
        out_specs=(vmem, vmem),
        scratch_shapes=[
            like(positions),
            like(features),
            like(lever),
            like(body_slot),
            like(owner_dir),
            like(body_pose),
            like(body_motion),
            like(body_inverse),
            like(weight_u),
            like(weight_v),
            pltpu.VMEM((100, 128, 128), BF16),
            pltpu.VMEM((100, 128, 128), BF16),
            pltpu.VMEM((100, 16, 128), BF16),
            pltpu.VMEM((64, 32, 128), BF16),
            pltpu.VMEM((64, 512, 128), BF16),
            pltpu.VMEM((64, 128, 128), BF16),
            pltpu.VMEM((512, 128), F32),
            pltpu.VMEM((512, 128), F32),
            pltpu.VMEM((144, 128), F32),
            pltpu.VMEM((9, 8, 128), F32),
            pltpu.VMEM((9, 8, 128), F32),
            pltpu.VMEM((576, 128), BF16),
            pltpu.VMEM((32, 128), F32),
            pltpu.VMEM((2, 8, 3, 128), BF16),
            pltpu.VMEM((2, 8, 3, 128), BF16),
            pltpu.VMEM((4, 3, 128), BF16),
            pltpu.VMEM((2, 8, 128, 128), BF16),
            pltpu.VMEM((2, 8, 128, 128), BF16),
            pltpu.VMEM((4, 128, 128), BF16),
            pltpu.VMEM((5, 768, 256), F32),
            pltpu.VMEM((5, 768, 256), F32),
            dma((24,)),
            dma((8,)),
            dma((8,)),
            dma((8,)),
            dma((8,)),
            dma((8,)),
            dma((8,)),
            dma((8,)),
            dma((8,)),
        ],
        compiler_params=pltpu.CompilerParams(
            collective_id=0, has_side_effects=True, vmem_limit_bytes=60 * 1024 * 1024
        ),
        name="step",
    )(
        partner,
        radial_rate,
        positions,
        features,
        lever,
        body_slot,
        owner_dir,
        body_pose,
        body_motion,
        body_inverse,
        weight_u,
        weight_v,
    )


def solution(mesh):
    tiles = P("gx", "gy", None, None)
    flat = P("gx", "gy", None)
    return jax.shard_map(
        local,
        mesh=mesh,
        in_specs=(tiles, tiles, tiles, flat, flat, flat, tiles, tiles, tiles, P(), P(), P()),
        out_specs=(tiles, tiles),
        check_vma=False,
    )
```

time: 684 us -> 74.9 us (0.11); the launches traced: 671 us -> 74.4 us
  local copies, waits for them, and re-layouts: 251 us -> 9.89 us
  other arithmetic: 177 us -> 0 us
  matrix products: 174 us -> 0 us
  Pallas kernels: 0 us -> 63.9 us
  starting transfers between devices: 29.6 us -> 0 us
  loops' own time: 22.9 us -> 0 us
  waiting for transfers between devices: 15.2 us -> 0 us
    dot_general x114 -> x0, matrix products: 174 us -> none  [the longest x48 74.7 us: tile_forces(): jnp.einsum('mkha,mhb->mkab', u_row, v_part, preferred_element_type=jnp.fl...]
    while x928 -> x0, local copies, waits for them, and re-layouts: 133 us -> none
    pallas_call x0 -> x1, Pallas kernels: none -> 63.9 us  [local(): pl.pallas_call(kernel, out_shape=(jax.ShapeDtypeStruct((8, 8, 3, 128), F3...]
    dynamic_slice x64 -> x0, local copies, waits for them, and re-layouts: 60.4 us -> none  [the longest x48 48.1 us: local(): lax.map(row_forces, (jnp.arange(tiles_x, dtype=jnp.int32), u_all.reshape(...]
    eq x120 -> x0, other arithmetic: 48.8 us -> none  [the longest x48 17.1 us: pick_partner(): sel_mid = (off_y == 0).reshape(shape_mask)]
    reduce_sum x63 -> x0, other arithmetic: 37.2 us -> none  [the longest x8 25.8 us: tile_forces(): radius_sq = jnp.sum(differ * differ, axis=1)]
    ppermute x12 -> x0, starting transfers between devices: 29.6 us -> none  [the longest x4 20.2 us: padded_2(): after = lax.ppermute(leading, axis, down)]
    select_n x16 -> x0, other arithmetic: 26.9 us -> none  [pick_partner(): jnp.where(sel_up, per_row[0], jnp.where(sel_same, per_row[1], per_row[2]))]
  transfers between devices with their start and end apart: 12 -> 0, of which waited for: 8 -> 0; matrix products, arithmetic and copies ran while one was open for 5% -> 0% of each run, Pallas kernels for 0% -> 0%
where the time goes in v1:
time: 74.9 us; the launch traced here: 74.4 us
  Pallas kernels  63.9 us (85%)
  local copies, waits for them, and re-layouts  9.89 us (13%)
    pallas_call x1, Pallas kernels, local(): pl.pallas_call(kernel, out_shape=(jax.ShapeDtypeStruct((8, 8, 3, 128), F3...  63.9 us
    unnamed x5, local copies, waits for them, and re-layouts  7.04 us
    pallas_call x2, local copies, waits for them, and re-layouts, local(): pl.pallas_call(kernel, out_shape=(jax.ShapeDtypeStruct((8, 8, 3, 128), F3...  2.85 us

profile of v1, /device:TPU:1, one launch (start us, length us, event | category | flops | bytes accessed | tf_op | source)
XLA Modules:
  0.0 74.4 jit_solution(52085611979996005)
XLA Ops:
  0.6 1.3 %copy.17.pose_in = f32[1,1,7,128]{3,2,1,0:T(8,128)} copy(f32[1,1,7,128]{3,1,2,0:T(1,128)} %param.18) | data formatting | bytes 7168 | tf_op args[6]
  1.9 1.3 %copy.18.motion_in = f32[1,1,6,128]{3,2,1,0:T(8,128)} copy(f32[1,1,6,128]{3,1,2,0:T(1,128)} %param.19) | data formatting | bytes 6144 | tf_op args[7]
  3.2 1.5 %copy.14.codes = s32[8,8,6]{2,1,0:T(8,128)} copy(s32[8,8,6]{1,0,2:T(8,128)} %param.15) | data formatting | bytes 3072 | tf_op args[3]
  4.6 1.5 %copy.15.positions = bf16[8,8,3,128]{3,2,1,0:T(4,128)(2,1)} copy(bf16[8,8,3,128]{3,1,2,0:T(8,128)(2,1)} %param.12) | data formatting | bytes 98304 | tf_op args[0]
  6.1 1.6 %copy.16.lever_in = f32[8,8,3,128]{3,2,1,0:T(4,128)} copy(f32[8,8,3,128]{3,1,2,0:T(8,128)} %param.14) | data formatting | bytes 196608 | tf_op args[2]
  7.7 63.9 %step.1 = (f32[8,8,3,128]{3,2,1,0:T(4,128)}, f32[1,1,13,128]{3,2,1,0:T(8,128)}) custom-call(s32[8,8,6]{2,1,0:T(8,128)} %copy.14.codes, f32[4]{0:T(128)} %rates.1, bf16[8,8,3,128]{3,2,1,0:T(4,128)(2,1)} %copy.15.positions, bf16[8,8,256,128]{3,2,1,0:T(8,128)(2,1)} %features.1, f32[8,8,3,128]{3,2,1,0:T(4,128)} %copy.16.lever_in, s32[8,8,128]{2,1,0:T(8,128)} %slot_in.1, ...), custom_call_target="tpu_custom_call" | custom-call | tf_op jit(solution)/shard_map/step/pallas_call | solution.py:706
  71.6 1.6 %copy.19 = f32[8,8,3,128]{3,1,2,0:T(8,128)} copy(f32[8,8,3,128]{3,2,1,0:T(4,128)} %get-tuple-element.2) | data formatting | bytes 196608 | tf_op jit(solution)/shard_map/step/pallas_call | solution.py:706
  73.1 1.3 %copy.20 = f32[1,1,13,128]{3,1,2,0:T(1,128)} copy(f32[1,1,13,128]{3,2,1,0:T(8,128)} %get-tuple-element.3) | data formatting | bytes 13312 | tf_op jit(solution)/shard_map/step/pallas_call | solution.py:706

commit v2 on v1

v2 whole, which is shorter than its diff:
```python
import jax
import jax.numpy as jnp
from jax import lax
from jax.experimental import pallas as pl
from jax.experimental.pallas import tpu as pltpu
from jax.sharding import PartitionSpec as P

STEP_DT = 0.25
LOG2E = 1.4426950408889634
MESH = pl.DeviceIdType.MESH
F32 = jnp.float32
BF16 = jnp.bfloat16
INNER_FIRST = 14
CODES = [c for c in range(9) if c != 4]
MIX = "DUUDUUDUUDUUDUU"


def mm(a, b):
    return jnp.dot(a, b, preferred_element_type=F32)


def mm_nt(a, b):
    return lax.dot_general(a, b, (((1,), (1,)), ((), ())), preferred_element_type=F32)


def split3(value):
    high = value.astype(BF16).astype(F32)
    rest = value - high
    mid = rest.astype(BF16).astype(F32)
    return high, mid, rest - mid


def inner_pair(q):
    i = 1 + q // 3
    j = 1 + 2 * (q % 3)
    return i, j, i, j + 1


def rim_pair(q):
    in_rows = q < 8
    c = q - 8
    i = jnp.where(in_rows, 7 * (q // 4), 1 + 2 * (c % 3))
    j = jnp.where(in_rows, 2 * (q % 4), 7 * (c // 3))
    return i, j, jnp.where(in_rows, i, i + 1), jnp.where(in_rows, j + 1, j)


def row_pair(q):
    i = 7 * (q // 4)
    j = 2 * (q % 4)
    return i, j, i, j + 1


def col_pair(q):
    i = 1 + 2 * (q % 3)
    j = 7 * (q // 3)
    return i, j, i + 1, j


def any_pair(p):
    rim = rim_pair(jnp.clip(p - INNER_FIRST, 0, 13))
    inner = inner_pair(jnp.clip(jnp.where(p < INNER_FIRST, p, p - 14), 0, 17))
    is_rim = (p >= INNER_FIRST) & (p < INNER_FIRST + 14)
    return tuple(jnp.where(is_rim, r, n) for r, n in zip(rim, inner))


def rotation_rows(qw, qa, qb, qc):
    return [
        [1 - 2 * (qb * qb + qc * qc), 2 * (qa * qb - qw * qc), 2 * (qa * qc + qw * qb)],
        [2 * (qa * qb + qw * qc), 1 - 2 * (qa * qa + qc * qc), 2 * (qb * qc - qw * qa)],
        [2 * (qa * qc - qw * qb), 2 * (qb * qc + qw * qa), 1 - 2 * (qa * qa + qb * qb)],
    ]


def kernel(
    codes,
    rates,
    positions,
    features,
    lever_in,
    slot_in,
    owner_in,
    pose_in,
    motion_in,
    inverse_in,
    wu_in,
    wv_in,
    moved,
    body_next,
    pos,
    feat,
    lever,
    slot,
    owner,
    pose,
    motion,
    inverse,
    wu,
    wv,
    vt,
    qf,
    qm,
    rp,
    u,
    oh,
    raw,
    terms,
    picked,
    acc,
    part_out,
    part_in,
    table,
    table_f32,
    pos32,
    stage_q,
    stage_r,
    stage_m,
    pos_row,
    pos_col,
    pos_corner,
    v_row,
    v_col,
    v_corner,
    s_even,
    s_odd,
    in_sem,
    pos_send,
    pos_recv,
    v_send,
    v_recv,
    part_send,
    part_recv,
    table_send,
    table_recv,
):
    gx, gy = lax.axis_index("gx"), lax.axis_index("gy")
    nx, ny = lax.axis_size("gx"), lax.axis_size("gy")

    def neighbour(code):
        a, b = code // 3 - 1, code % 3 - 1
        return (lax.rem(gx + a + nx, nx), lax.rem(gy + b + ny, ny))

    loads = []

    def load(src, dst):
        copy = pltpu.make_async_copy(src, dst, in_sem.at[len(loads)])
        copy.start()
        loads.append(copy)
        return copy

    got_pos = load(positions, pos)
    got_wv = load(wv_in, wv)
    rim_loads = [
        load(features.at[0], feat.at[0]),
        load(features.at[7], feat.at[7]),
        load(features.at[1:7, 0], feat.at[1:7, 0]),
        load(features.at[1:7, 7], feat.at[1:7, 7]),
    ]
    small_loads = [
        load(slot_in, slot),
        load(owner_in, owner),
        load(lever_in, lever),
        load(pose_in, pose),
        load(motion_in, motion),
        load(inverse_in, inverse),
        load(wu_in, wu),
    ]
    inner_loads = [load(features.at[i, 1:7], feat.at[i, 1:7]) for i in range(1, 7)]

    barrier = pltpu.get_barrier_semaphore()
    for code in CODES:
        pl.semaphore_signal(barrier, inc=1, device_id=neighbour(code), device_id_type=MESH)

    rate_scale = [rates[k] * (-LOG2E) for k in range(4)]
    lead = rate_scale[0]
    ratio = [None] + [rate_scale[k] / lead for k in range(1, 4)]
    four_lead = -4.0 * lead
    final_scale = 1.0 / (2048.0 * lead * lead)
    raw[...] = jnp.zeros_like(raw)
    acc[...] = jnp.zeros_like(acc)
    stage_q[...] = jnp.zeros_like(stage_q)
    stage_r[...] = jnp.zeros_like(stage_r)
    stage_m[...] = jnp.zeros_like(stage_m)
    table_f32[...] = jnp.zeros_like(table_f32)

    got_pos.wait()
    pos32[...] = pos[...].astype(F32)
    pl.semaphore_wait(barrier, 8)

    def v_src(a, b):
        if b == 0:
            return vt.at[pl.ds(11 if a < 0 else 81, 8)]
        if a == 0:
            return None
        return vt.at[(10 if a < 0 else 80) + (1 if b < 0 else 8)]

    def landing(a, b, row_ref, col_ref, corner_ref):
        if b == 0:
            return row_ref.at[1 if a < 0 else 0]
        if a == 0:
            return col_ref.at[1 if b < 0 else 0]
        return corner_ref.at[(2 if a < 0 else 0) + (1 if b < 0 else 0)]

    pos_copies, v_copies = [], []

    def send_pos(src, dst, code):
        n = len(pos_copies)
        copy = pltpu.make_async_remote_copy(
            src_ref=src,
            dst_ref=dst,
            send_sem=pos_send.at[n],
            recv_sem=pos_recv.at[n],
            device_id=neighbour(code),
            device_id_type=MESH,
        )
        copy.start()
        pos_copies.append(copy)

    for code in CODES:
        a, b = code // 3 - 1, code % 3 - 1
        i, j = (0 if a < 0 else 7), (0 if b < 0 else 7)
        if b == 0:
            send_pos(pos32.at[i], pos_row.at[1 if a < 0 else 0], code)
        elif a == 0:
            for c in range(3):
                send_pos(pos32.at[:, c, j], pos_col.at[1 if b < 0 else 0, c], code)
        else:
            k = (2 if a < 0 else 0) + (1 if b < 0 else 0)
            send_pos(pos32.at[i, :, j], pos_corner.at[:, k], code)

    lane = lax.broadcasted_iota(jnp.int32, (128, 128), 1)
    own_lanes = [jnp.where(lane // 32 == m, 1.0, 0.0).astype(BF16) for m in range(4)]
    zero8 = jnp.zeros((8, 128), F32)
    one8 = jnp.ones((8, 128), F32)
    steps8 = lax.broadcasted_iota(jnp.int32, (8, 128), 0).astype(F32) - 3.5

    def place(i):
        return jnp.full((8, 128), i.astype(F32) - 3.5)

    def put_rows(ref, stride, values):
        for r, value in enumerate(values):
            ref[pl.ds(r, 8, stride=stride), :] = value

    def partner_tables(q, gi, gj, indices):
        ax, ay = q[0] + gi, q[1] + gj
        square = split3(lead * (ax * ax + ay * ay + q[2] * q[2]))
        values = [q[0]] * 3 + [q[1]] * 3 + [q[2]] * 3 + [gi] * 3 + [gj] * 3
        put_rows(stage_q, 32, values + list(square) + [one8] * 3)
        put_rows(stage_m, 8, [q[0], q[1], q[2], one8, gi, gj])
        for half in range((len(indices) + 3) // 4):
            turned = stage_q[128 * half : 128 * half + 128, :].T.astype(BF16)
            for m, index in enumerate(indices[4 * half : 4 * half + 4]):
                qf[index] = turned * own_lanes[m]
        for m, index in enumerate(indices):
            rows = stage_m[8 * m : 8 * m + 8, :]
            qm[index] = jnp.concatenate([rows, zero8], axis=0).astype(BF16)

    slots = lax.broadcasted_iota(jnp.int32, (128, 128), 0)
    for copy in small_loads:
        copy.wait()

    def prepare(i, carry):
        q = [pos32[i, c] for c in range(3)]
        gi = place(i)
        partner_tables(q, gi, steps8, [(i + 1) * 10 + 1 + m for m in range(8)])
        ax, ay, az = q[0] + gi, q[1] + steps8, q[2]
        xs = list(split3(-2.0 * lead * ax))
        ys = list(split3(-2.0 * lead * ay))
        zs = list(split3(-2.0 * lead * az))
        sq = list(split3(lead * (ax * ax + ay * ay + az * az)))
        put_rows(stage_r, 32, xs + ys + zs + xs + ys + [one8] * 3 + sq)
        for m in range(8):
            rp[i * 8 + m] = stage_r[32 * m : 32 * m + 32, :].astype(BF16)
            here = slot[i, m : m + 1, :]
            oh[i * 8 + m] = jnp.where(slots == here, 1.0, 0.0).astype(BF16)
        return carry

    lax.fori_loop(0, 8, prepare, 0)

    def project(pair, want_v, want_u):
        ia, ja, ib, jb = pair
        both = jnp.concatenate([feat[ia, ja], feat[ib, jb]], axis=1)
        if want_v:
            v = mm(wv[...], both).astype(BF16)
            vt[(ia + 1) * 10 + ja + 1] = v[:, 0:128].T
            vt[(ib + 1) * 10 + jb + 1] = v[:, 128:256].T
        if want_u:
            all_u = mm(wu[...], both).astype(BF16)
            u[ia * 8 + ja] = all_u[:, 0:128]
            u[ib * 8 + jb] = all_u[:, 128:256]

    got_wv.wait()
    for copy in rim_loads:
        copy.wait()

    def rim_v(q, carry):
        project(rim_pair(2 * q), True, False)
        project(rim_pair(2 * q + 1), True, False)
        return carry

    lax.fori_loop(0, 7, rim_v, 0)

    vt4 = vt.reshape(10, 10, 128, 128)
    for n, code in enumerate(CODES):
        a, b = code // 3 - 1, code % 3 - 1
        src = vt4.at[1:9, 1 if b < 0 else 8] if a == 0 else v_src(a, b)
        v_copies.append(
            pltpu.make_async_remote_copy(
                src_ref=src,
                dst_ref=landing(a, b, v_row, v_col, v_corner),
                send_sem=v_send.at[n],
                recv_sem=v_recv.at[n],
                device_id=neighbour(code),
                device_id_type=MESH,
            )
        )
    for n in sorted(range(8), key=lambda n: (CODES[n] // 3 == 1, CODES[n])):
        v_copies[n].start()

    for copy in inner_loads:
        copy.wait()

    def inner_rows(q, carry):
        for step in range(3):
            project(inner_pair(3 * q + step), True, True)
        return carry

    def rim_u(q, carry):
        project(rim_pair(2 * q), False, True)
        project(rim_pair(2 * q + 1), False, True)
        return carry

    lax.fori_loop(0, 6, inner_rows, 0)
    lax.fori_loop(0, 7, rim_u, 0)

    def where_is(p):
        ia, ja, ib, jb = any_pair(p)
        found = [ia * 8 + ja, ib * 8 + jb]
        for i, j in ((ia, ja), (ib, jb)):
            for n in range(6):
                c = codes[n, i, j]
                found.append(i * 10 + j + c + 7 * ((c * 11) >> 5))
        return tuple(found)

    zeros128 = jnp.zeros((128, 128), BF16)

    def scores(at, s):
        for x in range(2):
            rows = jnp.concatenate([vt[n] for n in at[2 + 6 * x : 8 + 6 * x]], axis=0)
            for half in range(2):
                first = u[at[x], 256 * half : 256 * half + 128, :]
                second = u[at[x], 256 * half + 128 : 256 * half + 256, :]
                s[2 * x + half] = mm(rows, jnp.concatenate([first, second], axis=1))
                yield
        rows = jnp.concatenate(
            [jnp.concatenate([qf[n], qf[m]], axis=1) for n, m in zip(at[2:8], at[8:14])], axis=0
        )
        right = jnp.concatenate(
            [
                jnp.concatenate([rp[at[0]]] * 4 + [zeros128], axis=0),
                jnp.concatenate([zeros128] + [rp[at[1]]] * 4, axis=0),
            ],
            axis=1,
        )
        s[4] = mm(rows, right)
        yield

    def couples(at, s):
        for x in range(2):
            t, found = at[x], at[2 + 6 * x : 8 + 6 * x]
            total = None
            for two in range(3):
                couple = []
                for n in (2 * two, 2 * two + 1):
                    rows = slice(n * 128, (n + 1) * 128)
                    t0 = s[4, rows, x * 128 : (x + 1) * 128]
                    mixed = None
                    for k in range(4):
                        score = s[2 * x + k // 2, rows, (k % 2) * 128 : (k % 2 + 1) * 128]
                        term = jnp.exp2(t0 if k == 0 else t0 * ratio[k]) * score
                        mixed = term if mixed is None else mixed + term
                    inside = jnp.maximum(t0 + four_lead, 0.0)
                    couple.append((mixed * (inside * inside)).astype(BF16))
                    yield
                left = jnp.concatenate([qm[found[2 * two]], qm[found[2 * two + 1]]], axis=1)
                got = mm(left, jnp.concatenate(couple, axis=0))
                total = got if total is None else total + got
            raw[pl.ds(pl.multiple_of(t * 8, 8), 8), :] = total[0:8]

    def run(steps):
        for _ in steps:
            pass

    def mixed_run(first, second):
        for which in MIX:
            next(first if which == "D" else second)
        run(first)
        run(second)

    def finish_halo():
        for copy in pos_copies:
            copy.wait_recv()
        for copy in v_copies:
            copy.wait_recv()

        def rows(side, carry):
            edge = place(9 * side - 1)
            at = [90 * side + 1 + m for m in range(8)]
            for m in range(8):
                vt[at[m]] = v_row[side, m]
            partner_tables([pos_row[side, c] for c in range(3)], edge, steps8, at)
            return carry

        def cols(side, carry):
            edge = place(9 * side - 1)
            at = [(m + 1) * 10 + 9 * side for m in range(8)]
            for m in range(8):
                vt[at[m]] = v_col[side, m]
            partner_tables([pos_col[side, c] for c in range(3)], steps8, edge, at)
            return carry

        lax.fori_loop(0, 2, rows, 0)
        lax.fori_loop(0, 2, cols, 0)
        k = lax.broadcasted_iota(jnp.int32, (8, 128), 0)
        gi = jnp.where(k < 2, -4.5, 4.5)
        gj = jnp.where(k % 2 == 0, -4.5, 4.5)
        at = [0, 9, 90, 99]
        for m in range(4):
            vt[at[m]] = v_corner[m]
        partner_tables([pos_corner[c] for c in range(3)], gi, gj, at)

    def force_terms():
        def row(i, carry):
            def strided(c):
                return raw[pl.ds(64 * i + c, 8, stride=8), :]

            weight = strided(3)
            px, py, pz = pos32[i, 0] + place(i), pos32[i, 1] + steps8, pos32[i, 2]
            lx, ly, lz = lever[i, 0], lever[i, 1], lever[i, 2]
            fx = (px * weight - (strided(0) + strided(4))) * final_scale
            fy = (py * weight - (strided(1) + strided(5))) * final_scale
            fz = (pz * weight - strided(2)) * final_scale
            rows = [fx, fy, fz, ly * fz - lz * fy, lz * fx - lx * fz, lx * fy - ly * fx]
            put = rows + [zero8] * 2
            for c, value in enumerate(put):
                high = value.astype(BF16).astype(F32)
                terms[pl.ds(128 * i + c, 8, stride=16), :] = high
                terms[pl.ds(128 * i + 8 + c, 8, stride=16), :] = value - high
            return carry

        lax.fori_loop(0, 8, row, 0)

    def part_terms(t):
        return terms[pl.ds(pl.multiple_of(t * 16, 16), 16), :]

    def masked_sums(places, start, count):
        left, right = [], []
        for i, j in places:
            t = i * 8 + j
            value = part_terms(t)
            whose = owner[i, pl.ds(j, 1), :]
            masks = [jnp.where(whose == start + c, value, 0.0) for c in range(count)]
            left.append(jnp.concatenate(masks, axis=0).astype(BF16))
            right.append(oh[t])
        got = mm_nt(jnp.concatenate(left, axis=1), jnp.concatenate(right, axis=1))
        where = pl.ds(pl.multiple_of(start * 16, 16), count * 16)
        acc[where, :] = acc[where, :] + got

    part_copies = []
    for n, code in enumerate(CODES):
        part_copies.append(
            pltpu.make_async_remote_copy(
                src_ref=part_out.at[code],
                dst_ref=part_in.at[code],
                send_sem=part_send.at[n],
                recv_sem=part_recv.at[n],
                device_id=neighbour(code),
                device_id_type=MESH,
            )
        )

    def send_parts():
        force_terms()

        def rows(side, carry):
            masked_sums([(7 * side, m) for m in range(8)], 3 * side, 6)
            return carry

        def cols(side, carry):
            masked_sums([(m, 7 * side) for m in range(1, 7)], 3 + side, 2)
            return carry

        lax.fori_loop(0, 2, rows, 0)
        lax.fori_loop(0, 2, cols, 0)
        for code in CODES:
            part_out[code] = acc[16 * code : 16 * code + 8, :] + acc[16 * code + 8 : 16 * code + 16, :]
        for copy in part_copies:
            copy.start()

    first = where_is(jnp.int32(0))
    run(scores(first, s_even))

    def two_pairs(q, carry):
        now, after = carry[:14], carry[14:]
        pl.when(q == INNER_FIRST // 2 - 1)(finish_halo)
        pl.when(q == INNER_FIRST // 2 + 7)(send_parts)
        later = where_is(2 * q + 2)
        last = where_is(2 * q + 3)
        mixed_run(scores(after, s_odd), couples(now, s_even))
        mixed_run(scores(later, s_even), couples(after, s_odd))
        return later + last

    carry = lax.fori_loop(0, 15, two_pairs, first + where_is(jnp.int32(1)))
    now, after = carry[:14], carry[14:]
    mixed_run(scores(after, s_odd), couples(now, s_even))
    run(couples(after, s_odd))

    force_terms()

    def inner_sums(q, total):
        left, right = [], []
        for i in (2 * q + 1, 2 * q + 2):
            for j in range(1, 7):
                left.append(part_terms(i * 8 + j).astype(BF16))
                right.append(oh[i * 8 + j])
        return total + mm_nt(jnp.concatenate(left, axis=1), jnp.concatenate(right, axis=1))

    own = lax.fori_loop(0, 3, inner_sums, acc[64:80, :])
    total = own[0:8] + own[8:16]
    for copy in part_copies:
        copy.wait_recv()
    for code in CODES:
        total = total + part_in[code]

    inv = inverse[0, 0]
    centre = [pose[0, c] for c in range(3)]
    quat = [pose[0, c] for c in range(3, 7)]
    vel = [motion[0, c] + STEP_DT * inv[0:1] * total[c : c + 1] for c in range(3)]
    ang = [motion[0, c] + STEP_DT * total[c : c + 1] for c in range(3, 6)]
    shift = [STEP_DT * v for v in vel]
    rot = rotation_rows(*quat)
    frame = [
        (rot[0][c] * ang[0] + rot[1][c] * ang[1] + rot[2][c] * ang[2]) * inv[c + 1 : c + 2]
        for c in range(3)
    ]
    omega = [rot[r][0] * frame[0] + rot[r][1] * frame[1] + rot[r][2] * frame[2] for r in range(3)]
    qw, qv = quat[0], quat[1:4]
    change = [
        -(omega[0] * qv[0] + omega[1] * qv[1] + omega[2] * qv[2]),
        qw * omega[0] + (omega[1] * qv[2] - omega[2] * qv[1]),
        qw * omega[1] + (omega[2] * qv[0] - omega[0] * qv[2]),
        qw * omega[2] + (omega[0] * qv[1] - omega[1] * qv[0]),
    ]
    stepped = [q + 0.5 * STEP_DT * d for q, d in zip(quat, change)]
    norm = jnp.sqrt(sum(s * s for s in stepped[1:]) + stepped[0] * stepped[0])
    turned = [s / norm for s in stepped]
    rot_new = rotation_rows(*turned)
    for c in range(3):
        table_f32[c : c + 1, :] = shift[c]
        for r in range(3):
            entry = sum(rot_new[r][k] * rot[c][k] for k in range(3))
            table_f32[3 * (c + 1) + r : 3 * (c + 1) + r + 1, :] = entry
    whole = table_f32[...]
    high = whole.astype(BF16)
    table[128:144, :] = high
    table[144:160, :] = (whole - high.astype(F32)).astype(BF16)
    table_copies = []
    for n, code in enumerate(CODES):
        table_copies.append(
            pltpu.make_async_remote_copy(
                src_ref=table.at[pl.ds(128, 32)],
                dst_ref=table.at[pl.ds((8 - code) * 32, 32)],
                send_sem=table_send.at[n],
                recv_sem=table_recv.at[n],
                device_id=neighbour(code),
                device_id_type=MESH,
            )
        )
    for copy in table_copies:
        copy.start()
    next_rows = [c + s for c, s in zip(centre, shift)] + turned + vel + ang
    for c, value in enumerate(next_rows):
        body_next[0, c] = value

    def look_up(places, start, count):
        if count == 1:
            rows = table[128:160, :]
        else:
            rows = table[pl.ds(pl.multiple_of(start * 32, 32), count * 32), :]
        tiles = [i * 8 + j for i, j in places]
        got = mm(rows, jnp.concatenate([oh[t] for t in tiles], axis=1))
        for n, (i, j) in enumerate(places):
            lanes = slice(128 * n, 128 * n + 128)
            found = None
            for c in range(count):
                one = got[32 * c : 32 * c + 16, lanes] + got[32 * c + 16 : 32 * c + 32, lanes]
                if c:
                    whose = owner[i, pl.ds(j, 1), :]
                    found = jnp.where(whose == start + c, one, found)
                else:
                    found = one
            picked[pl.ds(pl.multiple_of(tiles[n] * 16, 16), 16), :] = found

    def look_inner(i, carry):
        look_up([(i, j) for j in range(1, 7)], 4, 1)
        return carry

    lax.fori_loop(1, 7, look_inner, 0)
    for copy in table_copies:
        copy.wait_recv()

    def look_rows(q, carry):
        i, start = 7 * (q // 2), 3 * (q // 2)
        look_up([(i, 4 * (q % 2) + m) for m in range(4)], start, 6)
        return carry

    def look_cols(side, carry):
        look_up([(i, 7 * side) for i in range(1, 7)], 3 + side, 2)
        return carry

    lax.fori_loop(0, 4, look_rows, 0)
    lax.fori_loop(0, 2, look_cols, 0)

    def move(i, carry):
        def strided(c):
            return picked[pl.ds(128 * i + c, 8, stride=16), :]

        levers = [lever[i, c] for c in range(3)]
        for r in range(3):
            value = pos32[i, r] + strided(r)
            for c in range(3):
                value = value + strided(3 + 3 * c + r) * levers[c]
            moved[i, r] = value - levers[r]
        return carry

    lax.fori_loop(0, 8, move, 0)
    for copy in pos_copies + v_copies + part_copies + table_copies:
        copy.wait_send()


def local(
    positions,
    features,
    lever,
    partner,
    body_slot,
    owner_dir,
    body_pose,
    body_motion,
    body_inverse,
    weight_u,
    weight_v,
    radial_rate,
):
    hbm = pl.BlockSpec(memory_space=pl.ANY)
    smem = pl.BlockSpec(memory_space=pltpu.SMEM)
    vmem = pl.BlockSpec(memory_space=pltpu.VMEM)
    dma = pltpu.SemaphoreType.DMA
    like = lambda x: pltpu.VMEM(x.shape, x.dtype)
    inside = lambda x: jnp.transpose(x, (0, 2, 1, 3))
    positions, lever = inside(positions), inside(lever)
    body_pose, body_motion = inside(body_pose), inside(body_motion)
    partner = jnp.transpose(partner, (2, 0, 1))
    moved, body_next = pl.pallas_call(
        kernel,
        out_shape=(
            jax.ShapeDtypeStruct((8, 3, 8, 128), F32),
            jax.ShapeDtypeStruct((1, 13, 1, 128), F32),
        ),
        in_specs=[smem, smem] + [hbm] * 10,
        out_specs=(vmem, vmem),
        scratch_shapes=[
            like(positions),
            like(features),
            like(lever),
            like(body_slot),
            like(owner_dir),
            like(body_pose),
            like(body_motion),
            like(body_inverse),
            like(weight_u),
            like(weight_v),
            pltpu.VMEM((100, 128, 128), BF16),
            pltpu.VMEM((100, 128, 128), BF16),
            pltpu.VMEM((100, 16, 128), BF16),
            pltpu.VMEM((64, 32, 128), BF16),
            pltpu.VMEM((64, 512, 128), BF16),
            pltpu.VMEM((64, 128, 128), BF16),
            pltpu.VMEM((512, 128), F32),
            pltpu.VMEM((1024, 128), F32),
            pltpu.VMEM((1024, 128), F32),
            pltpu.VMEM((144, 128), F32),
            pltpu.VMEM((9, 8, 128), F32),
            pltpu.VMEM((9, 8, 128), F32),
            pltpu.VMEM((288, 128), BF16),
            pltpu.VMEM((16, 128), F32),
            pltpu.VMEM((8, 3, 8, 128), F32),
            pltpu.VMEM((256, 128), F32),
            pltpu.VMEM((256, 128), F32),
            pltpu.VMEM((64, 128), F32),
            pltpu.VMEM((2, 3, 8, 128), F32),
            pltpu.VMEM((2, 3, 8, 128), F32),
            pltpu.VMEM((3, 8, 128), F32),
            pltpu.VMEM((2, 8, 128, 128), BF16),
            pltpu.VMEM((2, 8, 128, 128), BF16),
            pltpu.VMEM((4, 128, 128), BF16),
            pltpu.VMEM((5, 768, 256), F32),
            pltpu.VMEM((5, 768, 256), F32),
            dma((24,)),
            dma((12,)),
            dma((12,)),
            dma((8,)),
            dma((8,)),
            dma((8,)),
            dma((8,)),
            dma((8,)),
            dma((8,)),
        ],
        compiler_params=pltpu.CompilerParams(
            collective_id=0, has_side_effects=True, vmem_limit_bytes=60 * 1024 * 1024
        ),
        name="step",
    )(
        partner,
        radial_rate,
        positions,
        features,
        lever,
        body_slot,
        owner_dir,
        body_pose,
        body_motion,
        body_inverse,
        weight_u,
        weight_v,
    )
    return inside(moved), inside(body_next)


def solution(mesh):
    tiles = P("gx", "gy", None, None)
    flat = P("gx", "gy", None)
    return jax.shard_map(
        local,
        mesh=mesh,
        in_specs=(tiles, tiles, tiles, flat, flat, flat, tiles, tiles, tiles, P(), P(), P()),
        out_specs=(tiles, tiles),
        check_vma=False,
    )
```

time: 74.9 us -> 58.6 us (0.78)
  Pallas kernels: 63.9 us -> 54.9 us
  local copies, waits for them, and re-layouts: 9.89 us -> 2.83 us
    pallas_call x1, Pallas kernels: 63.9 us -> 54.9 us  [local(): pl.pallas_call(kernel, out_shape=(jax.ShapeDtypeStruct((8, 3, 8, 128), F3...]
    unnamed x5 -> x2, local copies, waits for them, and re-layouts: 7.04 us -> 2.83 us
    pallas_call x2 -> x0, local copies, waits for them, and re-layouts: 2.85 us -> none  [local(): pl.pallas_call(kernel, out_shape=(jax.ShapeDtypeStruct((8, 8, 3, 128), F3...]
where the time goes in v2:
time: 58.6 us; the launch traced here: 58.3 us
  Pallas kernels  54.9 us (94%)
  local copies, waits for them, and re-layouts  2.83 us (5%)
  between operations  0.64 us (1%)
    pallas_call x1, Pallas kernels, local(): pl.pallas_call(kernel, out_shape=(jax.ShapeDtypeStruct((8, 3, 8, 128), F3...  54.9 us
    unnamed x2, local copies, waits for them, and re-layouts  2.83 us

profile of v2, /device:TPU:1, one launch (start us, length us, event | category | flops | bytes accessed | tf_op | source)
XLA Modules:
  0.0 58.3 jit_solution(16302840172051810318)
XLA Ops:
  0.6 54.9 %step.1 = (f32[8,3,8,128]{3,2,1,0:T(8,128)}, f32[1,13,1,128]{3,2,1,0:T(1,128)}) custom-call(s32[6,8,8]{2,1,0:T(8,128)} %bitcast.12, f32[4]{0:T(128)} %rates.1, bf16[8,3,8,128]{3,2,1,0:T(8,128)(2,1)} %bitcast.11, bf16[8,8,256,128]{3,2,1,0:T(8,128)(2,1)} %features.1, f32[8,3,8,128]{3,2,1,0:T(8,128)} %bitcast.10, s32[8,8,128]{2,1,0:T(8,128)} %slot_in.1, ...), custom_call_target="tpu_custom_call" | custom-call | tf_op jit(solution)/shard_map/step/pallas_call | solution.py:663
  55.5 1.5 %copy.17 = f32[8,8,3,128]{3,1,2,0:T(8,128)} copy(f32[8,8,3,128]{3,1,2,0:T(8,128)} %bitcast.9) | data formatting | bytes 196608
  57.1 1.3 %copy.18 = f32[1,1,13,128]{3,1,2,0:T(1,128)} copy(f32[1,1,13,128]{3,1,2,0:T(1,128)} %bitcast.13) | data formatting | bytes 13312

commit v3 on v2

--- a/solution.py
+++ b/solution.py
@@ -13,6 +13,7 @@
 INNER_FIRST = 14
 CODES = [c for c in range(9) if c != 4]
 MIX = "DUUDUUDUUDUUDUU"
+DOTS = (0, 1, 4, 2, 3)
 
 
 def mm(a, b):
@@ -184,7 +185,6 @@
 
     got_pos.wait()
     pos32[...] = pos[...].astype(F32)
-    pl.semaphore_wait(barrier, 8)
 
     def v_src(a, b):
         if b == 0:
@@ -199,33 +199,6 @@
         if a == 0:
             return col_ref.at[1 if b < 0 else 0]
         return corner_ref.at[(2 if a < 0 else 0) + (1 if b < 0 else 0)]
-
-    pos_copies, v_copies = [], []
-
-    def send_pos(src, dst, code):
-        n = len(pos_copies)
-        copy = pltpu.make_async_remote_copy(
-            src_ref=src,
-            dst_ref=dst,
-            send_sem=pos_send.at[n],
-            recv_sem=pos_recv.at[n],
-            device_id=neighbour(code),
-            device_id_type=MESH,
-        )
-        copy.start()
-        pos_copies.append(copy)
-
-    for code in CODES:
-        a, b = code // 3 - 1, code % 3 - 1
-        i, j = (0 if a < 0 else 7), (0 if b < 0 else 7)
-        if b == 0:
-            send_pos(pos32.at[i], pos_row.at[1 if a < 0 else 0], code)
-        elif a == 0:
-            for c in range(3):
-                send_pos(pos32.at[:, c, j], pos_col.at[1 if b < 0 else 0, c], code)
-        else:
-            k = (2 if a < 0 else 0) + (1 if b < 0 else 0)
-            send_pos(pos32.at[i, :, j], pos_corner.at[:, k], code)
 
     lane = lax.broadcasted_iota(jnp.int32, (128, 128), 1)
     own_lanes = [jnp.where(lane // 32 == m, 1.0, 0.0).astype(BF16) for m in range(4)]
@@ -298,6 +271,34 @@
         return carry
 
     lax.fori_loop(0, 7, rim_v, 0)
+
+    pl.semaphore_wait(barrier, 8)
+    pos_copies, v_copies = [], []
+
+    def send_pos(src, dst, code):
+        n = len(pos_copies)
+        copy = pltpu.make_async_remote_copy(
+            src_ref=src,
+            dst_ref=dst,
+            send_sem=pos_send.at[n],
+            recv_sem=pos_recv.at[n],
+            device_id=neighbour(code),
+            device_id_type=MESH,
+        )
+        copy.start()
+        pos_copies.append(copy)
+
+    for code in CODES:
+        a, b = code // 3 - 1, code % 3 - 1
+        i, j = (0 if a < 0 else 7), (0 if b < 0 else 7)
+        if b == 0:
+            send_pos(pos32.at[i], pos_row.at[1 if a < 0 else 0], code)
+        elif a == 0:
+            for c in range(3):
+                send_pos(pos32.at[:, c, j], pos_col.at[1 if b < 0 else 0, c], code)
+        else:
+            k = (2 if a < 0 else 0) + (1 if b < 0 else 0)
+            send_pos(pos32.at[i, :, j], pos_corner.at[:, k], code)
 
     vt4 = vt.reshape(10, 10, 128, 128)
     for n, code in enumerate(CODES):
@@ -344,25 +345,24 @@
     zeros128 = jnp.zeros((128, 128), BF16)
 
     def scores(at, s):
-        for x in range(2):
-            rows = jnp.concatenate([vt[n] for n in at[2 + 6 * x : 8 + 6 * x]], axis=0)
-            for half in range(2):
+        for which in DOTS:
+            if which == 4:
+                rows = [jnp.concatenate([qf[n], qf[m]], axis=1) for n, m in zip(at[2:8], at[8:14])]
+                right = jnp.concatenate(
+                    [
+                        jnp.concatenate([rp[at[0]]] * 4 + [zeros128], axis=0),
+                        jnp.concatenate([zeros128] + [rp[at[1]]] * 4, axis=0),
+                    ],
+                    axis=1,
+                )
+            else:
+                x, half = which // 2, which % 2
+                rows = [vt[n] for n in at[2 + 6 * x : 8 + 6 * x]]
                 first = u[at[x], 256 * half : 256 * half + 128, :]
                 second = u[at[x], 256 * half + 128 : 256 * half + 256, :]
-                s[2 * x + half] = mm(rows, jnp.concatenate([first, second], axis=1))
-                yield
-        rows = jnp.concatenate(
-            [jnp.concatenate([qf[n], qf[m]], axis=1) for n, m in zip(at[2:8], at[8:14])], axis=0
-        )
-        right = jnp.concatenate(
-            [
-                jnp.concatenate([rp[at[0]]] * 4 + [zeros128], axis=0),
-                jnp.concatenate([zeros128] + [rp[at[1]]] * 4, axis=0),
-            ],
-            axis=1,
-        )
-        s[4] = mm(rows, right)
-        yield
+                right = jnp.concatenate([first, second], axis=1)
+            s[which] = mm(jnp.concatenate(rows, axis=0), right)
+            yield
 
     def couples(at, s):
         for x in range(2):

time: 58.6 us -> 56.5 us (0.964)
  Pallas kernels: 54.9 us -> 52.8 us
    pallas_call x1, Pallas kernels: 54.9 us -> 52.8 us  [local(): pl.pallas_call(kernel, out_shape=(jax.ShapeDtypeStruct((8, 3, 8, 128), F3...]
where the time goes in v3:
time: 56.5 us; the launch traced here: 56.2 us
  Pallas kernels  52.8 us (93%)
  local copies, waits for them, and re-layouts  2.83 us (5%)
  between operations  0.64 us (1%)
    pallas_call x1, Pallas kernels, local(): pl.pallas_call(kernel, out_shape=(jax.ShapeDtypeStruct((8, 3, 8, 128), F3...  52.8 us
    unnamed x2, local copies, waits for them, and re-layouts  2.83 us

profile of v3, /device:TPU:1, one launch (start us, length us, event | category | flops | bytes accessed | tf_op | source)
XLA Modules:
  0.0 56.2 jit_solution(15683670953094132227)
XLA Ops:
  0.6 52.8 %step.1 = (f32[8,3,8,128]{3,2,1,0:T(8,128)}, f32[1,13,1,128]{3,2,1,0:T(1,128)}) custom-call(s32[6,8,8]{2,1,0:T(8,128)} %bitcast.12, f32[4]{0:T(128)} %rates.1, bf16[8,3,8,128]{3,2,1,0:T(8,128)(2,1)} %bitcast.11, bf16[8,8,256,128]{3,2,1,0:T(8,128)(2,1)} %features.1, f32[8,3,8,128]{3,2,1,0:T(8,128)} %bitcast.10, s32[8,8,128]{2,1,0:T(8,128)} %slot_in.1, ...), custom_call_target="tpu_custom_call" | custom-call | tf_op jit(solution)/shard_map/step/pallas_call | solution.py:663
  53.4 1.5 %copy.17 = f32[8,8,3,128]{3,1,2,0:T(8,128)} copy(f32[8,8,3,128]{3,1,2,0:T(8,128)} %bitcast.9) | data formatting | bytes 196608
  54.9 1.3 %copy.18 = f32[1,1,13,128]{3,1,2,0:T(1,128)} copy(f32[1,1,13,128]{3,1,2,0:T(1,128)} %bitcast.13) | data formatting | bytes 13312

commit v4 on v3

--- a/solution.py
+++ b/solution.py
@@ -55,6 +55,12 @@
     i = 1 + 2 * (q % 3)
     j = 7 * (q // 3)
     return i, j, i + 1, j
+
+
+def rim_then_inner(p):
+    rim = rim_pair(jnp.clip(p, 0, 13))
+    inner = inner_pair(jnp.clip(p - 14, 0, 17))
+    return tuple(jnp.where(p < 14, r, n) for r, n in zip(rim, inner))
 
 
 def any_pair(p):
@@ -95,8 +101,7 @@
     pose,
     motion,
     inverse,
-    wu,
-    wv,
+    weights,
     vt,
     qf,
     qm,
@@ -149,7 +154,7 @@
         return copy
 
     got_pos = load(positions, pos)
-    got_wv = load(wv_in, wv)
+    got_weights = [load(wu_in, weights.at[0:512]), load(wv_in, weights.at[512:640])]
     rim_loads = [
         load(features.at[0], feat.at[0]),
         load(features.at[7], feat.at[7]),
@@ -163,7 +168,6 @@
         load(pose_in, pose),
         load(motion_in, motion),
         load(inverse_in, inverse),
-        load(wu_in, wu),
     ]
     inner_loads = [load(features.at[i, 1:7], feat.at[i, 1:7]) for i in range(1, 7)]
 
@@ -249,31 +253,34 @@
 
     lax.fori_loop(0, 8, prepare, 0)
 
-    def project(pair, want_v, want_u):
+    pos_copies, v_copies = [], []
+
+    def project(pair, s):
         ia, ja, ib, jb = pair
         both = jnp.concatenate([feat[ia, ja], feat[ib, jb]], axis=1)
-        if want_v:
-            v = mm(wv[...], both).astype(BF16)
-            vt[(ia + 1) * 10 + ja + 1] = v[:, 0:128].T
-            vt[(ib + 1) * 10 + jb + 1] = v[:, 128:256].T
-        if want_u:
-            all_u = mm(wu[...], both).astype(BF16)
-            u[ia * 8 + ja] = all_u[:, 0:128]
-            u[ib * 8 + jb] = all_u[:, 128:256]
-
-    got_wv.wait()
-    for copy in rim_loads:
+        s[0, 0:640, :] = mm(weights[...], both)
+
+    def settle(pair, s):
+        ia, ja, ib, jb = pair
+        for i, j, lanes in ((ia, ja, slice(0, 128)), (ib, jb, slice(128, 256))):
+            u[i * 8 + j] = s[0, 0:512, lanes].astype(BF16)
+            vt[(i + 1) * 10 + j + 1] = s[0, 512:640, lanes].astype(BF16).T
+
+    for copy in got_weights + rim_loads + inner_loads:
         copy.wait()
-
-    def rim_v(q, carry):
-        project(rim_pair(2 * q), True, False)
-        project(rim_pair(2 * q + 1), True, False)
-        return carry
-
-    lax.fori_loop(0, 7, rim_v, 0)
-
+    start = [rim_then_inner(jnp.int32(p)) for p in range(3)]
+    project(start[0], s_even)
+
+    def project_two(q, carry):
+        now, after, later = carry
+        project(after, s_odd)
+        settle(now, s_even)
+        project(later, s_even)
+        settle(after, s_odd)
+        return later, rim_then_inner(2 * q + 3), rim_then_inner(2 * q + 4)
+
+    carry = lax.fori_loop(0, 7, project_two, tuple(start))
     pl.semaphore_wait(barrier, 8)
-    pos_copies, v_copies = [], []
 
     def send_pos(src, dst, code):
         n = len(pos_copies)
@@ -317,21 +324,7 @@
     for n in sorted(range(8), key=lambda n: (CODES[n] // 3 == 1, CODES[n])):
         v_copies[n].start()
 
-    for copy in inner_loads:
-        copy.wait()
-
-    def inner_rows(q, carry):
-        for step in range(3):
-            project(inner_pair(3 * q + step), True, True)
-        return carry
-
-    def rim_u(q, carry):
-        project(rim_pair(2 * q), False, True)
-        project(rim_pair(2 * q + 1), False, True)
-        return carry
-
-    lax.fori_loop(0, 6, inner_rows, 0)
-    lax.fori_loop(0, 7, rim_u, 0)
+    lax.fori_loop(7, 16, project_two, carry)
 
     def where_is(p):
         ia, ja, ib, jb = any_pair(p)
@@ -637,6 +630,17 @@
         copy.wait_send()
 
 
+def hand_over(moved, body_next, moved_out, body_out, sem):
+    copies = [
+        pltpu.make_async_copy(moved, moved_out, sem.at[0]),
+        pltpu.make_async_copy(body_next, body_out, sem.at[1]),
+    ]
+    for copy in copies:
+        copy.start()
+    for copy in copies:
+        copy.wait()
+
+
 def local(
     positions,
     features,
@@ -663,8 +667,8 @@
     moved, body_next = pl.pallas_call(
         kernel,
         out_shape=(
-            jax.ShapeDtypeStruct((8, 3, 8, 128), F32),
-            jax.ShapeDtypeStruct((1, 13, 1, 128), F32),
+            pltpu.VMEM((8, 3, 8, 128), F32),
+            pltpu.VMEM((1, 13, 1, 128), F32),
         ),
         in_specs=[smem, smem] + [hbm] * 10,
         out_specs=(vmem, vmem),
@@ -677,8 +681,7 @@
             like(body_pose),
             like(body_motion),
             like(body_inverse),
-            like(weight_u),
-            like(weight_v),
+            pltpu.VMEM((640, 256), BF16),
             pltpu.VMEM((100, 128, 128), BF16),
             pltpu.VMEM((100, 128, 128), BF16),
             pltpu.VMEM((100, 16, 128), BF16),
@@ -733,6 +736,20 @@
         weight_u,
         weight_v,
     )
+    moved, body_next = pl.pallas_call(
+        hand_over,
+        out_shape=(
+            jax.ShapeDtypeStruct((8, 3, 8, 128), F32),
+            jax.ShapeDtypeStruct((1, 13, 1, 128), F32),
+        ),
+        in_specs=[vmem, vmem],
+        out_specs=(hbm, hbm),
+        scratch_shapes=[dma((2,))],
+        name="out",
+    )(
+        pltpu.with_memory_space_constraint(moved, pltpu.VMEM),
+        pltpu.with_memory_space_constraint(body_next, pltpu.VMEM),
+    )
     return inside(moved), inside(body_next)
 
 

time: 56.5 us -> 53.4 us (0.945)
  local copies, waits for them, and re-layouts: 2.83 us -> 0 us
    unnamed x2 -> x0, local copies, waits for them, and re-layouts: 2.83 us -> none
    pallas_call x1 -> x2, Pallas kernels: 52.8 us -> 52.6 us  [the longest x1 51.9 us: local(): pl.pallas_call(kernel, out_shape=(pltpu.VMEM((8, 3, 8, 128), F32), pltpu....]
where the time goes in v4:
time: 53.4 us; the launch traced here: 53.2 us
  Pallas kernels  52.6 us (99%)
  between operations  0.64 us (1%)
    pallas_call x1, Pallas kernels, local(): pl.pallas_call(kernel, out_shape=(pltpu.VMEM((8, 3, 8, 128), F32), pltpu....  51.9 us

profile of v4, /device:TPU:1, one launch (start us, length us, event | category | flops | bytes accessed | tf_op | source)
XLA Modules:
  0.0 53.2 jit_solution(11318944713859566986)
XLA Ops:
  0.6 51.9 %step.1 = (f32[8,3,8,128]{3,2,1,0:T(8,128)S(1)}, f32[1,13,1,128]{3,2,1,0:T(1,128)S(1)}) custom-call(s32[6,8,8]{2,1,0:T(8,128)} %bitcast.11, f32[4]{0:T(128)} %rates.1, bf16[8,3,8,128]{3,2,1,0:T(8,128)(2,1)} %bitcast.10, bf16[8,8,256,128]{3,2,1,0:T(8,128)(2,1)} %features.1, f32[8,3,8,128]{3,2,1,0:T(8,128)} %bitcast.9, s32[8,8,128]{2,1,0:T(8,128)} %slot_in.1, ...), custom_call_target="tpu_custom_call" | custom-call | tf_op jit(solution)/shard_map/step/pallas_call | solution.py:667
  52.6 0.7 %out.1 = (f32[8,3,8,128]{3,2,1,0:T(8,128)}, f32[1,13,1,128]{3,2,1,0:T(1,128)}) custom-call(f32[8,3,8,128]{3,2,1,0:T(8,128)S(1)} %get-tuple-element.6.moved, f32[1,13,1,128]{3,2,1,0:T(1,128)S(1)} %get-tuple-element.7.body_next), custom_call_target="tpu_custom_call" | custom-call | tf_op jit(solution)/shard_map/out/pallas_call | solution.py:739

commit v5 on v4

--- a/solution.py
+++ b/solution.py
@@ -1,3 +1,5 @@
+import functools
+
 import jax
 import jax.numpy as jnp
 from jax import lax
@@ -235,7 +237,7 @@
     for copy in small_loads:
         copy.wait()
 
-    def prepare(i, carry):
+    def prepare(i):
         q = [pos32[i, c] for c in range(3)]
         gi = place(i)
         partner_tables(q, gi, steps8, [(i + 1) * 10 + 1 + m for m in range(8)])
@@ -249,37 +251,38 @@
             rp[i * 8 + m] = stage_r[32 * m : 32 * m + 32, :].astype(BF16)
             here = slot[i, m : m + 1, :]
             oh[i * 8 + m] = jnp.where(slots == here, 1.0, 0.0).astype(BF16)
-        return carry
-
-    lax.fori_loop(0, 8, prepare, 0)
+
 
     pos_copies, v_copies = [], []
+
+    buffers = [s_even.at[0], s_odd.at[0], s_even.at[1], s_odd.at[1]]
 
     def project(pair, s):
         ia, ja, ib, jb = pair
         both = jnp.concatenate([feat[ia, ja], feat[ib, jb]], axis=1)
-        s[0, 0:640, :] = mm(weights[...], both)
+        s[0:640, :] = mm(weights[...], both)
 
     def settle(pair, s):
         ia, ja, ib, jb = pair
         for i, j, lanes in ((ia, ja, slice(0, 128)), (ib, jb, slice(128, 256))):
-            u[i * 8 + j] = s[0, 0:512, lanes].astype(BF16)
-            vt[(i + 1) * 10 + j + 1] = s[0, 512:640, lanes].astype(BF16).T
+            u[i * 8 + j] = s[0:512, lanes].astype(BF16)
+            vt[(i + 1) * 10 + j + 1] = s[512:640, lanes].astype(BF16).T
 
     for copy in got_weights + rim_loads + inner_loads:
         copy.wait()
-    start = [rim_then_inner(jnp.int32(p)) for p in range(3)]
-    project(start[0], s_even)
-
-    def project_two(q, carry):
-        now, after, later = carry
-        project(after, s_odd)
-        settle(now, s_even)
-        project(later, s_even)
-        settle(after, s_odd)
-        return later, rim_then_inner(2 * q + 3), rim_then_inner(2 * q + 4)
-
-    carry = lax.fori_loop(0, 7, project_two, tuple(start))
+    start = [rim_then_inner(jnp.int32(p)) for p in range(5)]
+    project(start[0], buffers[0])
+
+    def project_four(q, carry, tables):
+        for step in range(4):
+            project(carry[step + 1], buffers[(step + 1) % 4])
+            settle(carry[step], buffers[step])
+            if tables and step % 2 == 0:
+                prepare(2 * (q - 4) + step // 2)
+        return carry[4:] + tuple(rim_then_inner(4 * q + p) for p in range(5, 9))
+
+    rim_part = functools.partial(project_four, tables=False)
+    carry = lax.fori_loop(0, 4, rim_part, tuple(start))
     pl.semaphore_wait(barrier, 8)
 
     def send_pos(src, dst, code):
@@ -324,7 +327,7 @@
     for n in sorted(range(8), key=lambda n: (CODES[n] // 3 == 1, CODES[n])):
         v_copies[n].start()
 
-    lax.fori_loop(7, 16, project_two, carry)
+    lax.fori_loop(4, 8, functools.partial(project_four, tables=True), carry)
 
     def where_is(p):
         ia, ja, ib, jb = any_pair(p)

time: 53.4 us -> 51.8 us (0.970)
  Pallas kernels: 52.6 us -> 50.9 us
    pallas_call x1, Pallas kernels: 51.9 us -> 50.3 us  [local(): pl.pallas_call(kernel, out_shape=(pltpu.VMEM((8, 3, 8, 128), F32), pltpu....]
where the time goes in v5:
time: 51.8 us; the launch traced here: 51.6 us
  Pallas kernels  50.9 us (98%)
  between operations  0.64 us (1%)
    pallas_call x1, Pallas kernels, local(): pl.pallas_call(kernel, out_shape=(pltpu.VMEM((8, 3, 8, 128), F32), pltpu....  50.3 us

profile of v5, /device:TPU:1, one launch (start us, length us, event | category | flops | bytes accessed | tf_op | source)
XLA Modules:
  0.0 51.6 jit_solution(2147767532029566004)
XLA Ops:
  0.6 50.3 %step.1 = (f32[8,3,8,128]{3,2,1,0:T(8,128)S(1)}, f32[1,13,1,128]{3,2,1,0:T(1,128)S(1)}) custom-call(s32[6,8,8]{2,1,0:T(8,128)} %bitcast.11, f32[4]{0:T(128)} %rates.1, bf16[8,3,8,128]{3,2,1,0:T(8,128)(2,1)} %bitcast.10, bf16[8,8,256,128]{3,2,1,0:T(8,128)(2,1)} %features.1, f32[8,3,8,128]{3,2,1,0:T(8,128)} %bitcast.9, s32[8,8,128]{2,1,0:T(8,128)} %slot_in.1, ...), custom_call_target="tpu_custom_call" | custom-call | tf_op jit(solution)/shard_map/step/pallas_call | solution.py:670
  50.9 0.7 %out.1 = (f32[8,3,8,128]{3,2,1,0:T(8,128)}, f32[1,13,1,128]{3,2,1,0:T(1,128)}) custom-call(f32[8,3,8,128]{3,2,1,0:T(8,128)S(1)} %get-tuple-element.6.moved, f32[1,13,1,128]{3,2,1,0:T(1,128)S(1)} %get-tuple-element.7.body_next), custom_call_target="tpu_custom_call" | custom-call | tf_op jit(solution)/shard_map/out/pallas_call | solution.py:742

commit v6 on v5

--- a/solution.py
+++ b/solution.py
@@ -15,7 +15,7 @@
 INNER_FIRST = 14
 CODES = [c for c in range(9) if c != 4]
 MIX = "DUUDUUDUUDUUDUU"
-DOTS = (0, 1, 4, 2, 3)
+DOTS = (0, 1, 2, 3, 4)
 
 
 def mm(a, b):
@@ -122,6 +122,7 @@
     stage_q,
     stage_r,
     stage_m,
+    stage_n,
     pos_row,
     pos_col,
     pos_corner,
@@ -187,6 +188,7 @@
     stage_q[...] = jnp.zeros_like(stage_q)
     stage_r[...] = jnp.zeros_like(stage_r)
     stage_m[...] = jnp.zeros_like(stage_m)
+    stage_n[...] = jnp.zeros_like(stage_n)
     table_f32[...] = jnp.zeros_like(table_f32)
 
     got_pos.wait()
@@ -219,18 +221,18 @@
         for r, value in enumerate(values):
             ref[pl.ds(r, 8, stride=stride), :] = value
 
-    def partner_tables(q, gi, gj, indices):
+    def partner_tables(q, gi, gj, indices, wide=stage_q, narrow=stage_m):
         ax, ay = q[0] + gi, q[1] + gj
         square = split3(lead * (ax * ax + ay * ay + q[2] * q[2]))
         values = [q[0]] * 3 + [q[1]] * 3 + [q[2]] * 3 + [gi] * 3 + [gj] * 3
-        put_rows(stage_q, 32, values + list(square) + [one8] * 3)
-        put_rows(stage_m, 8, [q[0], q[1], q[2], one8, gi, gj])
+        put_rows(wide, 32, values + list(square) + [one8] * 3)
+        put_rows(narrow, 8, [q[0], q[1], q[2], one8, gi, gj])
         for half in range((len(indices) + 3) // 4):
-            turned = stage_q[128 * half : 128 * half + 128, :].T.astype(BF16)
+            turned = wide[128 * half : 128 * half + 128, :].T.astype(BF16)
             for m, index in enumerate(indices[4 * half : 4 * half + 4]):
                 qf[index] = turned * own_lanes[m]
         for m, index in enumerate(indices):
-            rows = stage_m[8 * m : 8 * m + 8, :]
+            rows = narrow[8 * m : 8 * m + 8, :]
             qm[index] = jnp.concatenate([rows, zero8], axis=0).astype(BF16)
 
     slots = lax.broadcasted_iota(jnp.int32, (128, 128), 0)
@@ -268,7 +270,7 @@
             u[i * 8 + j] = s[0:512, lanes].astype(BF16)
             vt[(i + 1) * 10 + j + 1] = s[512:640, lanes].astype(BF16).T
 
-    for copy in got_weights + rim_loads + inner_loads:
+    for copy in got_weights + rim_loads + inner_loads[:1]:
         copy.wait()
     start = [rim_then_inner(jnp.int32(p)) for p in range(5)]
     project(start[0], buffers[0])
@@ -327,6 +329,8 @@
     for n in sorted(range(8), key=lambda n: (CODES[n] // 3 == 1, CODES[n])):
         v_copies[n].start()
 
+    for copy in inner_loads[1:]:
+        copy.wait()
     lax.fori_loop(4, 8, functools.partial(project_four, tables=True), carry)
 
     def where_is(p):
@@ -398,24 +402,20 @@
         for copy in v_copies:
             copy.wait_recv()
 
-        def rows(side, carry):
+        def sides(side, carry):
             edge = place(9 * side - 1)
-            at = [90 * side + 1 + m for m in range(8)]
+            in_row = [90 * side + 1 + m for m in range(8)]
+            in_col = [(m + 1) * 10 + 9 * side for m in range(8)]
+            along = [pos_row[side, c] for c in range(3)]
+            across = [pos_col[side, c] for c in range(3)]
+            partner_tables(along, edge, steps8, in_row)
+            partner_tables(across, steps8, edge, in_col, stage_r, stage_n)
             for m in range(8):
-                vt[at[m]] = v_row[side, m]
-            partner_tables([pos_row[side, c] for c in range(3)], edge, steps8, at)
+                vt[in_row[m]] = v_row[side, m]
+                vt[in_col[m]] = v_col[side, m]
             return carry
 
-        def cols(side, carry):
-            edge = place(9 * side - 1)
-            at = [(m + 1) * 10 + 9 * side for m in range(8)]
-            for m in range(8):
-                vt[at[m]] = v_col[side, m]
-            partner_tables([pos_col[side, c] for c in range(3)], steps8, edge, at)
-            return carry
-
-        lax.fori_loop(0, 2, rows, 0)
-        lax.fori_loop(0, 2, cols, 0)
+        lax.fori_loop(0, 2, sides, 0)
         k = lax.broadcasted_iota(jnp.int32, (8, 128), 0)
         gi = jnp.where(k < 2, -4.5, 4.5)
         gj = jnp.where(k % 2 == 0, -4.5, 4.5)
@@ -703,6 +703,7 @@
             pltpu.VMEM((256, 128), F32),
             pltpu.VMEM((256, 128), F32),
             pltpu.VMEM((64, 128), F32),
+            pltpu.VMEM((64, 128), F32),
             pltpu.VMEM((2, 3, 8, 128), F32),
             pltpu.VMEM((2, 3, 8, 128), F32),
             pltpu.VMEM((3, 8, 128), F32),

time: 51.8 us -> 50.8 us (0.981)
  Pallas kernels: 50.9 us -> 50 us
    pallas_call x1, Pallas kernels: 50.3 us -> 49.3 us  [local(): pl.pallas_call(kernel, out_shape=(pltpu.VMEM((8, 3, 8, 128), F32), pltpu....]
where the time goes in v6:
time: 50.8 us; the launch traced here: 50.6 us
  Pallas kernels  50 us (98%)
  between operations  0.64 us (1%)
    pallas_call x1, Pallas kernels, local(): pl.pallas_call(kernel, out_shape=(pltpu.VMEM((8, 3, 8, 128), F32), pltpu....  49.3 us

profile of v6, /device:TPU:1, one launch (start us, length us, event | category | flops | bytes accessed | tf_op | source)
XLA Modules:
  0.0 50.6 jit_solution(7893941694554520080)
XLA Ops:
  0.6 49.3 %step.1 = (f32[8,3,8,128]{3,2,1,0:T(8,128)S(1)}, f32[1,13,1,128]{3,2,1,0:T(1,128)S(1)}) custom-call(s32[6,8,8]{2,1,0:T(8,128)} %bitcast.11, f32[4]{0:T(128)} %rates.1, bf16[8,3,8,128]{3,2,1,0:T(8,128)(2,1)} %bitcast.10, bf16[8,8,256,128]{3,2,1,0:T(8,128)(2,1)} %features.1, f32[8,3,8,128]{3,2,1,0:T(8,128)} %bitcast.9, s32[8,8,128]{2,1,0:T(8,128)} %slot_in.1, ...), custom_call_target="tpu_custom_call" | custom-call | tf_op jit(solution)/shard_map/step/pallas_call | solution.py:670
  50.0 0.7 %out.1 = (f32[8,3,8,128]{3,2,1,0:T(8,128)}, f32[1,13,1,128]{3,2,1,0:T(1,128)}) custom-call(f32[8,3,8,128]{3,2,1,0:T(8,128)S(1)} %get-tuple-element.6.moved, f32[1,13,1,128]{3,2,1,0:T(1,128)S(1)} %get-tuple-element.7.body_next), custom_call_target="tpu_custom_call" | custom-call | tf_op jit(solution)/shard_map/out/pallas_call | solution.py:743

commit v7 on v6

--- a/solution.py
+++ b/solution.py
@@ -12,7 +12,7 @@
 MESH = pl.DeviceIdType.MESH
 F32 = jnp.float32
 BF16 = jnp.bfloat16
-INNER_FIRST = 14
+INNER_FIRST = 13
 CODES = [c for c in range(9) if c != 4]
 MIX = "DUUDUUDUUDUUDUU"
 DOTS = (0, 1, 2, 3, 4)
@@ -495,17 +495,26 @@
     first = where_is(jnp.int32(0))
     run(scores(first, s_even))
 
-    def two_pairs(q, carry):
+    def four_pairs(q, carry):
+        pl.when(q == 3)(finish_halo)
+        at = [carry[14 * n : 14 * n + 14] for n in range(2)]
+        at += [where_is(4 * q + n) for n in range(2, 6)]
+        for n in range(4):
+            filled, used = (s_odd, s_even) if n % 2 == 0 else (s_even, s_odd)
+            mixed_run(scores(at[n + 1], filled), couples(at[n], used))
+        return at[4] + at[5]
+
+    carry = lax.fori_loop(0, 7, four_pairs, first + where_is(jnp.int32(1)))
+    send_parts()
+
+    def last_pairs(q, carry):
         now, after = carry[:14], carry[14:]
-        pl.when(q == INNER_FIRST // 2 - 1)(finish_halo)
-        pl.when(q == INNER_FIRST // 2 + 7)(send_parts)
-        later = where_is(2 * q + 2)
-        last = where_is(2 * q + 3)
+        later, last = where_is(30 + 2 * q), where_is(31 + 2 * q)
         mixed_run(scores(after, s_odd), couples(now, s_even))
         mixed_run(scores(later, s_even), couples(after, s_odd))
         return later + last
 
-    carry = lax.fori_loop(0, 15, two_pairs, first + where_is(jnp.int32(1)))
+    carry = lax.fori_loop(0, 1, last_pairs, carry)
     now, after = carry[:14], carry[14:]
     mixed_run(scores(after, s_odd), couples(now, s_even))
     run(couples(after, s_odd))

time: 50.8 us -> 50.2 us (0.988)
  Pallas kernels: 50 us -> 49.4 us
    pallas_call x1, Pallas kernels: 49.3 us -> 48.7 us  [local(): pl.pallas_call(kernel, out_shape=(pltpu.VMEM((8, 3, 8, 128), F32), pltpu....]
where the time goes in v7:
time: 50.2 us; the launch traced here: 50 us
  Pallas kernels  49.4 us (98%)
  between operations  0.64 us (1%)
    pallas_call x1, Pallas kernels, local(): pl.pallas_call(kernel, out_shape=(pltpu.VMEM((8, 3, 8, 128), F32), pltpu....  48.7 us

profile of v7, /device:TPU:1, one launch (start us, length us, event | category | flops | bytes accessed | tf_op | source)
XLA Modules:
  0.0 50.0 jit_solution(940932857288198908)
XLA Ops:
  0.6 48.7 %step.1 = (f32[8,3,8,128]{3,2,1,0:T(8,128)S(1)}, f32[1,13,1,128]{3,2,1,0:T(1,128)S(1)}) custom-call(s32[6,8,8]{2,1,0:T(8,128)} %bitcast.11, f32[4]{0:T(128)} %rates.1, bf16[8,3,8,128]{3,2,1,0:T(8,128)(2,1)} %bitcast.10, bf16[8,8,256,128]{3,2,1,0:T(8,128)(2,1)} %features.1, f32[8,3,8,128]{3,2,1,0:T(8,128)} %bitcast.9, s32[8,8,128]{2,1,0:T(8,128)} %slot_in.1, ...), custom_call_target="tpu_custom_call" | custom-call | tf_op jit(solution)/shard_map/step/pallas_call | solution.py:679
  49.4 0.7 %out.1 = (f32[8,3,8,128]{3,2,1,0:T(8,128)}, f32[1,13,1,128]{3,2,1,0:T(1,128)}) custom-call(f32[8,3,8,128]{3,2,1,0:T(8,128)S(1)} %get-tuple-element.6.moved, f32[1,13,1,128]{3,2,1,0:T(1,128)S(1)} %get-tuple-element.7.body_next), custom_call_target="tpu_custom_call" | custom-call | tf_op jit(solution)/shard_map/out/pallas_call | solution.py:752

commit v8 on v7

--- a/solution.py
+++ b/solution.py
@@ -531,6 +531,7 @@
 
     own = lax.fori_loop(0, 3, inner_sums, acc[64:80, :])
     total = own[0:8] + own[8:16]
+    rot = rotation_rows(*[pose[0, c] for c in range(3, 7)])
     for copy in part_copies:
         copy.wait_recv()
     for code in CODES:
@@ -542,7 +543,6 @@
     vel = [motion[0, c] + STEP_DT * inv[0:1] * total[c : c + 1] for c in range(3)]
     ang = [motion[0, c] + STEP_DT * total[c : c + 1] for c in range(3, 6)]
     shift = [STEP_DT * v for v in vel]
-    rot = rotation_rows(*quat)
     frame = [
         (rot[0][c] * ang[0] + rot[1][c] * ang[1] + rot[2][c] * ang[2]) * inv[c + 1 : c + 2]
         for c in range(3)
@@ -614,15 +614,14 @@
         copy.wait_recv()
 
     def look_rows(q, carry):
-        i, start = 7 * (q // 2), 3 * (q // 2)
-        look_up([(i, 4 * (q % 2) + m) for m in range(4)], start, 6)
+        look_up([(7 * q, m) for m in range(8)], 3 * q, 6)
         return carry
 
     def look_cols(side, carry):
         look_up([(i, 7 * side) for i in range(1, 7)], 3 + side, 2)
         return carry
 
-    lax.fori_loop(0, 4, look_rows, 0)
+    lax.fori_loop(0, 2, look_rows, 0)
     lax.fori_loop(0, 2, look_cols, 0)
 
     def move(i, carry):

time: 50.2 us -> 50 us (level)
  no operation moved by 1% of the time
where the time goes in v8:
time: 50 us; the launch traced here: 49.8 us
  Pallas kernels  49.1 us (98%)
  between operations  0.64 us (1%)
    pallas_call x1, Pallas kernels, local(): pl.pallas_call(kernel, out_shape=(pltpu.VMEM((8, 3, 8, 128), F32), pltpu....  48.5 us

profile of v8, /device:TPU:1, one launch (start us, length us, event | category | flops | bytes accessed | tf_op | source)
XLA Modules:
  0.0 49.8 jit_solution(11368468717680694425)
XLA Ops:
  0.6 48.5 %step.1 = (f32[8,3,8,128]{3,2,1,0:T(8,128)S(1)}, f32[1,13,1,128]{3,2,1,0:T(1,128)S(1)}) custom-call(s32[6,8,8]{2,1,0:T(8,128)} %bitcast.11, f32[4]{0:T(128)} %rates.1, bf16[8,3,8,128]{3,2,1,0:T(8,128)(2,1)} %bitcast.10, bf16[8,8,256,128]{3,2,1,0:T(8,128)(2,1)} %features.1, f32[8,3,8,128]{3,2,1,0:T(8,128)} %bitcast.9, s32[8,8,128]{2,1,0:T(8,128)} %slot_in.1, ...), custom_call_target="tpu_custom_call" | custom-call | tf_op jit(solution)/shard_map/step/pallas_call | solution.py:678
  49.1 0.7 %out.1 = (f32[8,3,8,128]{3,2,1,0:T(8,128)}, f32[1,13,1,128]{3,2,1,0:T(1,128)}) custom-call(f32[8,3,8,128]{3,2,1,0:T(8,128)S(1)} %get-tuple-element.6.moved, f32[1,13,1,128]{3,2,1,0:T(1,128)S(1)} %get-tuple-element.7.body_next), custom_call_target="tpu_custom_call" | custom-call | tf_op jit(solution)/shard_map/out/pallas_call | solution.py:751
